TPU v7x, 128 devices: a whole 4x4x4 slice. The times are simulated.
128 devices in a mesh: rows: 4 (over y_lo, core), cols: 32 (over y_hi, z, x).
Axes of the slice: x: 4, y: 4 (y_hi: 2, y_lo: 2; y = y_hi * 2 + y_lo), z: 4, core: 2. Of those that a mesh axis runs over, the one named last changes fastest.
Arguments:
- features: bfloat16 [128, 1024, 512], P('rows', 'cols'), may hold values from -8 to 8
- dw_kernel: bfloat16 [13, 13, 512], replicated, may hold values from -0.5 to 0.5
- batchnorm_gain: float32 [512], replicated, may hold values from 0.1 to 1.9
- batchnorm_offset: float32 [512], replicated, may hold values from -3 to 3
- w_in: bfloat16 [512, 2048], replicated, may hold values from -0.25 to 0.25
- b_in: float32 [2048], replicated, may hold values from -3 to 3
- w_out: bfloat16 [2048, 512], replicated, may hold values from -0.125 to 0.125
- b_out: float32 [512], replicated, may hold values from -3 to 3
- layer_scale: float32 [512], replicated, may hold values from 0.25 to 1
- w_down: bfloat16 [2, 2, 512, 1024], replicated, may hold values from -0.125 to 0.125
- b_down: float32 [1024], replicated, may hold values from -3 to 3
- cotangent: bfloat16 [1024, 64, 512], P('cols', 'rows'), may hold values from -6 to 6
Outputs:
- coarse: bfloat16 [1024, 64, 512], P('cols', 'rows')
- grad_input: bfloat16 [128, 1024, 512], P('rows', 'cols')
- grad_kernel: float32 [13, 13, 512], replicated
All inputs are finite; a program needn't handle non-finite values.
Results may differ from a plain program's by a relative error of at most 0.0095.
Values may be sent and summed in bfloat16 or wider, within the bound.
A program may use at most 128 MiB of HBM per device.

v0:
```python
import functools

import jax
import jax.numpy as jnp
import numpy as np
from jax import lax
from jax.experimental import pallas as pl
from jax.experimental.pallas import tpu as pltpu
from jax.sharding import PartitionSpec as P

MESH = pl.DeviceIdType.MESH
F32 = jnp.float32
BF16 = jnp.bfloat16
NEAR_X = 4
GROUP = 8
HALF = 1024
CHUNK = 256


def balanced(table):
    low = table.astype(jnp.bfloat16)
    bits = low.view(np.uint16)
    up = (bits + 1).astype(np.uint16).view(jnp.bfloat16).astype(np.float64)
    down = (bits - 1).astype(np.uint16).view(jnp.bfloat16).astype(np.float64)
    value = low.astype(np.float64)
    out = value.copy()
    for row in range(table.shape[0]):
        excess = (value[row] - table[row]).sum()
        if excess == 0.0:
            continue
        live = np.nonzero(np.abs(table[row]) > 0.004)[0]
        steps = np.stack([up[row, live], down[row, live]]) - value[row, live]
        order = np.argsort(-np.abs(steps[0]), kind="stable")
        for spot in order:
            for step in steps[:, spot]:
                if abs(excess + step) < abs(excess) - 0.25 * abs(step):
                    out[row, live[spot]] += step
                    excess += step
                    break
    return out.astype(jnp.bfloat16)


@functools.lru_cache(maxsize=None)
def dft_tables(tile_h, tile_w, radius):
    nh, nw = tile_h + 2 * radius, tile_w + 2 * radius
    u, v, weight = np.zeros(HALF), np.zeros(HALF), np.zeros(HALF)
    index = 0
    for a in range(nh):
        for b in range(nw // 2 + 1):
            edge = b in (0, nw // 2)
            if edge and a > nh // 2:
                continue
            u[index], v[index] = a, b
            weight[index] = 1.0 if edge and a in (0, nh // 2) else 2.0
            index += 1
    live = weight > 0

    def rows(points):
        p = np.asarray(points)
        turns = (np.outer(u, p[:, 0]) % nh) / nh + (np.outer(v, p[:, 1]) % nw) / nw
        angle = 2.0 * np.pi * turns
        table = np.concatenate([np.cos(angle) * live[:, None], -np.sin(angle) * live[:, None]])
        table[np.abs(table) < 1e-9] = 0.0
        return table

    inner = [(h, w) for h in range(tile_h) for w in range(tile_w)]
    wests = range(-GROUP, 0)
    easts = range(tile_w, tile_w + GROUP)
    norths = range(-radius, 0)
    souths = range(tile_h, tile_h + radius)
    rim = [(h, w) for hs in (norths, souths) for h in hs for w in range(tile_w)]
    rim += [(h, w) for ws in (wests, easts) for h in range(tile_h) for w in ws]
    rim += [(h, w) for hs in (norths, souths) for ws in (wests, easts) for h in hs for w in ws]
    kept = np.asarray([-radius <= w < tile_w + radius for _, w in rim])
    taps = [(i, j) for i in range(-radius, radius + 1) for j in range(-radius, radius + 1)]
    both = balanced(np.concatenate([rows(inner), rows(rim) * kept[None]], axis=1))
    count = len(inner)
    tap_t = rows(taps)
    doubled = np.concatenate([weight, weight])[None]
    f_tap = np.pad(tap_t, ((0, 0), (0, CHUNK - len(taps)))).astype(jnp.bfloat16)
    f_out = (rows(inner).T * doubled).astype(jnp.bfloat16)
    tap_lines = -(-len(taps) // 48) * 48
    g_tap = np.pad(tap_t.T * doubled, ((0, tap_lines - len(taps)), (0, 0))).astype(jnp.bfloat16)
    return both[:, :count], both[:, count:], f_tap, f_out, g_tap


@functools.lru_cache(maxsize=None)
def phase_table(tile_w):
    table = np.zeros((CHUNK, CHUNK), np.float32)
    lines = CHUNK // tile_w
    for h in range(lines):
        for w in range(tile_w):
            plane = (h % 2) * 2 + w % 2
            table[plane * 64 + (h // 2) * (tile_w // 2) + w // 2, h * tile_w + w] = 1.0
    return table.astype(jnp.bfloat16)


def fdot(a, b):
    return jnp.dot(a, b, preferred_element_type=F32)


def ndot(a, b):
    return lax.dot_general(a, b, (((1,), (1,)), ((), ())), preferred_element_type=F32)


def rows_of(step, size=CHUNK):
    return pl.ds(pl.multiple_of(step * size, size), size)


def swap_blocks(parts):
    lane = lax.broadcasted_iota(jnp.int32, parts[0].shape, 1) // 16
    parts = list(parts)
    for k in (1, 2, 4):
        low = (lane // k) % 2 == 0
        for i in range(8):
            if i & k:
                continue
            a, b = parts[i], parts[i | k]
            parts[i] = jnp.where(low, a, pltpu.roll(b, 16 * k, 1))
            parts[i | k] = jnp.where(low, pltpu.roll(a, 128 - 16 * k, 1), b)
    return parts


class Place:
    def __init__(self, rows, cols):
        self.rows, self.cols = rows, cols
        self.r, self.c = lax.axis_index("rows"), lax.axis_index("cols")
        self.x, self.far = self.c % NEAR_X, self.c // NEAR_X
        self.fars, self.nears = cols // NEAR_X, rows * NEAR_X
        self.near = self.r * NEAR_X + self.x

    def near_dev(self, k):
        peer = (self.near + k) % self.nears
        return peer, {"rows": peer // NEAR_X, "cols": self.far * NEAR_X + peer % NEAR_X}

    def far_dev(self, k):
        peer = (self.far + k) % self.fars
        return peer, {"rows": self.r, "cols": peer * NEAR_X + self.x}

    def col_dev(self, k):
        peer = (self.c + k) % self.cols
        return peer, {"rows": self.r, "cols": peer}

    def inside(self, dr, dc):
        r, c = self.r + dr, self.c + dc
        return (r >= 0) & (r < self.rows) & (c >= 0) & (c < self.cols)

    def rim_dev(self, dr, dc):
        return {"rows": self.r + dr, "cols": self.c + dc}

    def greet(self):
        barrier = pltpu.get_barrier_semaphore()
        for dr, dc in STEPS:
            @pl.when(self.inside(dr, dc))
            def _():
                pl.semaphore_signal(
                    barrier, inc=1, device_id=self.rim_dev(dr, dc), device_id_type=MESH
                )
        for count, dev in (
            (self.nears, self.near_dev), (self.fars, self.far_dev), (self.cols, self.col_dev)
        ):
            for k in range(1, count):
                pl.semaphore_signal(barrier, inc=1, device_id=dev(k)[1], device_id_type=MESH)

    def met(self):
        def beside(at, size):
            return 1 + (at + size - 1) // size + (2 * size - 2 - at) // size

        around = beside(self.r, self.rows) * beside(self.c, self.cols) - 1
        pl.semaphore_wait(
            pltpu.get_barrier_semaphore(), around + self.nears + self.fars + self.cols - 3
        )


STEPS = ((1, 0), (-1, 0), (0, 1), (0, -1), (1, 1), (1, -1), (-1, 1), (-1, -1))


def send(src, dst, sems, slot, dev):
    pltpu.make_async_remote_copy(
        src, dst, sems.at[slot], sems.at[slot + 1], device_id=dev, device_id_type=MESH
    ).start()


def take(ref, sem):
    pltpu.make_async_copy(ref, ref, sem).wait()


def rim_pieces(block, radius, tb, lr, corner):
    lines, groups = block.shape[0], block.shape[1]
    south, north = pl.ds(lines - radius, radius), pl.ds(0, radius)
    last = groups - 1
    return (
        (block.at[south], tb.at[0]),
        (block.at[north], tb.at[1]),
        (block.at[:, last], lr.at[0]),
        (block.at[:, 0], lr.at[1]),
        (block.at[south, last], corner.at[0]),
        (block.at[south, 0], corner.at[1]),
        (block.at[north, last], corner.at[2]),
        (block.at[north, 0], corner.at[3]),
    )


def start_rim(place, pieces, sems):
    for (dr, dc), (src, dst), k in zip(STEPS, pieces, range(8)):
        @pl.when(place.inside(dr, dc))
        def _():
            send(src, dst, sems, 2 * k, place.rim_dev(dr, dc))


def finish_rim(place, pieces, sems, tb, lr, corner, rim):
    for (dr, dc), (_, dst), k in zip(STEPS, pieces, range(8)):
        @pl.when(place.inside(-dr, -dc))
        def _():
            take(dst, sems.at[2 * k + 1])

        @pl.when(jnp.logical_not(place.inside(-dr, -dc)))
        def _():
            dst[...] = jnp.zeros(dst.shape, BF16)

    channels = rim.shape[1]
    at = 0
    for ref in (tb, lr, corner):
        count = int(np.prod(ref.shape[:-1]))
        flat = ref[...].astype(F32).reshape(count, channels).astype(BF16)
        rim[at : at + count] = flat
        at += count


def drain_rim(place, pieces, sems):
    for (dr, dc), (_, dst), k in zip(STEPS, pieces, range(8)):
        @pl.when(place.inside(dr, dc))
        def _():
            take(dst, sems.at[2 * k])


def lines_of(row):
    return jnp.concatenate([row[:, k * 128 : (k + 1) * 128] for k in range(row.shape[1] // 128)], 0)


def row_of(lines):
    return jnp.concatenate([lines[k : k + 1] for k in range(lines.shape[0])], 1)


def merge_moments(buf, count, each):
    half = buf.shape[1] // 2
    means = buf[:, :half]
    mean = jnp.sum(means, axis=0) * (1.0 / count)
    gap = means - mean[None]
    spread = jnp.sum(buf[:, half:], axis=0) + each * jnp.sum(gap * gap, axis=0)
    return jnp.concatenate([mean, spread], axis=0)


def forward_kernel(
    rows, cols, radius,
    feat_hbm, feat4_hbm, cot_hbm, tap_hbm, fin_hbm, frim_hbm, ftap_hbm, fout_hbm, down_hbm, phase_hbm,
    conv_ref, spec_ref, moments_ref, grad_ref,
    feat, cot, taps, fin, frim, ftap, fout, down, phase,
    cot32, spread, cot_in, tap_spec, mixed, tb, lr, corner, rim, planes,
    near_buf, far_buf, mine, mid, in_sems, rim_sems, sems,
):
    place = Place(rows, cols)
    loads = [
        pltpu.make_async_copy(src, dst, in_sems.at[k])
        for k, (src, dst) in enumerate((
            (cot_hbm, cot), (tap_hbm, taps), (ftap_hbm, ftap), (feat_hbm, feat), (fin_hbm, fin),
            (frim_hbm, frim), (fout_hbm, fout), (down_hbm, down), (phase_hbm, phase),
        ))
    ]
    for load in loads:
        load.start()
    place.greet()

    loads[0].wait()
    outs, lines, width = cot.shape
    for tg in range(width // 128):
        cot32[tg] = cot[:, :, tg * 128 : (tg + 1) * 128].astype(F32).reshape(outs * lines, 128)
        for pg in range(lines // 8):
            parts = swap_blocks([
                cot32[tg, pl.ds(pg * 8 + k, outs, stride=lines), :] for k in range(8)
            ])
            for k in range(8):
                spread[tg * 8 + k, :, pg * 128 : (pg + 1) * 128] = parts[k].astype(BF16)
    place.met()
    pieces = rim_pieces(feat4_hbm, radius, tb, lr, corner)
    start_rim(place, pieces, rim_sems)
    for k in range(1, cols):
        peer, dev = place.col_dev(k)
        send(spread.at[peer], cot_in.at[place.c], sems, 0, dev)
    cot_in[place.c] = spread[place.c]

    loads[1].wait()
    loads[2].wait()

    @pl.loop(0, 2 * HALF // CHUNK)
    def _(m):
        tap_spec[rows_of(m)] = fdot(ftap[rows_of(m)], taps[...])

    loads[3].wait()
    loads[4].wait()

    @pl.loop(0, 2 * HALF // CHUNK)
    def _(m):
        spec_ref[rows_of(m)] = fdot(fin[rows_of(m)], feat[...])

    finish_rim(place, pieces, rim_sems, tb, lr, corner, rim)
    loads[5].wait()

    @pl.loop(0, HALF // CHUNK)
    def _(m):
        re, im = rows_of(m), rows_of(m + HALF // CHUNK)
        fr = spec_ref[re] + fdot(frim[re], rim[...])
        fi = spec_ref[im] + fdot(frim[im], rim[...])
        spec_ref[re], spec_ref[im] = fr, fi
        kr, ki = tap_spec[re], tap_spec[im]
        mixed[re] = (fr * kr + fi * ki).astype(BF16)
        mixed[im] = (fi * kr - fr * ki).astype(BF16)

    loads[6].wait()
    pixels = conv_ref.shape[0]
    channels = conv_ref.shape[1]
    area = (lines * 2 + 2 * radius) * (pixels // (lines * 2) + 2 * radius)

    def invert(m, total):
        block = fdot(fout[rows_of(m)], mixed[...]) * (1.0 / area)
        conv_ref[rows_of(m)] = block
        return total + jnp.sum(block, axis=0, keepdims=True)

    zero = jnp.zeros((1, channels), F32)
    mean = lax.fori_loop(0, pixels // CHUNK, invert, zero) * (1.0 / pixels)

    def scatter(m, total):
        gap = conv_ref[rows_of(m)] - mean
        return total + jnp.sum(gap * gap, axis=0, keepdims=True)

    around = lax.fori_loop(0, pixels // CHUNK, scatter, zero)
    mine[...] = jnp.concatenate([lines_of(mean), lines_of(around)], axis=0)
    for k in range(1, place.nears):
        send(mine, near_buf.at[place.near], sems, 2, place.near_dev(k)[1])
    near_buf[place.near] = mine[...]

    take(cot_in.at[pl.ds(0, cols - 1)], sems.at[1])
    loads[7].wait()
    loads[8].wait()
    tall = cot_in[...].reshape(cols * outs, lines * lines).astype(F32).T.astype(BF16)
    for ab in range(4):
        plane = ndot(tall, down[ab]).astype(BF16)
        for k in range(pixels // CHUNK):
            planes[k, ab * 64 : (ab + 1) * 64] = plane[k * 64 : (k + 1) * 64]
    take(near_buf.at[pl.ds(0, place.nears - 1)], sems.at[3])
    mid[...] = merge_moments(near_buf, place.nears, float(pixels))
    for k in range(1, place.fars):
        send(mid, far_buf.at[place.far], sems, 4, place.far_dev(k)[1])
    far_buf[place.far] = mid[...]
    for k in range(pixels // CHUNK):
        grad_ref[k * CHUNK : (k + 1) * CHUNK] = lax.dot_general(
            phase[...], planes[k], (((0,), (0,)), ((), ())), preferred_element_type=F32
        ).astype(BF16)
    take(far_buf.at[pl.ds(0, place.fars - 1)], sems.at[5])
    moments_ref[...] = merge_moments(far_buf, place.fars, float(pixels * place.nears))
    drain_rim(place, pieces, rim_sems)
    take(cot_in.at[pl.ds(0, cols - 1)], sems.at[0])
    take(near_buf.at[pl.ds(0, place.nears - 1)], sems.at[2])
    take(far_buf.at[pl.ds(0, place.fars - 1)], sems.at[4])


def forward_part(features, cotangent, dw_kernel, w_down):
    rows, cols = lax.axis_size("rows"), lax.axis_size("cols")
    tile_h, tile_w, channels = features.shape
    radius = (dw_kernel.shape[0] - 1) // 2
    pixels = tile_h * tile_w
    fin, frim, ftap, fout, _ = dft_tables(tile_h, tile_w, radius)
    groups = tile_w // GROUP
    taps = dw_kernel.reshape(-1, channels)
    taps = jnp.pad(taps, ((0, CHUNK - taps.shape[0]), (0, 0)))
    outs, lines, width = cotangent.shape
    operands = (
        features.reshape(pixels, channels),
        features.reshape(tile_h, groups, GROUP, channels),
        cotangent,
        taps,
        jnp.asarray(fin), jnp.asarray(frim), jnp.asarray(ftap), jnp.asarray(fout),
        w_down.reshape(4, channels, w_down.shape[-1]),
        jnp.asarray(phase_table(tile_w)),
    )
    stats_shape = (2 * channels // 128, 128)
    vm = pltpu.VMEM
    scratch = [vm(operands[k].shape, BF16) for k in (0, 2, 3, 4, 5, 6, 7, 8, 9)]
    scratch += [
        vm((width // 128, outs * lines, 128), F32),
        vm((cols, outs, lines * lines), BF16),
        vm((cols, outs, lines * lines), BF16),
        vm((2 * HALF, channels), F32),
        vm((2 * HALF, channels), BF16),
        vm((2, radius, groups, GROUP, channels), BF16),
        vm((2, tile_h, GROUP, channels), BF16),
        vm((4, radius, GROUP, channels), BF16),
        vm((frim.shape[1], channels), BF16),
        vm((pixels // CHUNK, CHUNK, channels), BF16),
        vm((rows * NEAR_X,) + stats_shape, F32),
        vm((cols // NEAR_X,) + stats_shape, F32),
        vm(stats_shape, F32),
        vm(stats_shape, F32),
        pltpu.SemaphoreType.DMA((9,)),
        pltpu.SemaphoreType.DMA((16,)),
        pltpu.SemaphoreType.DMA((6,)),
    ]
    return pl.pallas_call(
        functools.partial(forward_kernel, rows, cols, radius),
        out_shape=(
            jax.ShapeDtypeStruct((pixels, channels), F32),
            jax.ShapeDtypeStruct((2 * HALF, channels), F32),
            jax.ShapeDtypeStruct(stats_shape, F32),
            jax.ShapeDtypeStruct((pixels, channels), BF16),
        ),
        in_specs=[pl.BlockSpec(memory_space=pl.ANY)] * len(operands),
        out_specs=[pl.BlockSpec(memory_space=pltpu.VMEM)] * 4,
        scratch_shapes=scratch,
        compiler_params=pltpu.CompilerParams(
            collective_id=1, has_side_effects=True, vmem_limit_bytes=60 << 20
        ),
        name="forward_part",
    )(*operands)


def group_ids(rows, cols):
    r, c = lax.axis_index("rows"), lax.axis_index("cols")
    x, far = c % NEAR_X, c // NEAR_X
    fars = cols // NEAR_X
    near = r * NEAR_X + x
    return r, x, far, fars, near, rows * NEAR_X


def near_dev(index, far):
    return {"rows": index // NEAR_X, "cols": far * NEAR_X + index % NEAR_X}


def far_dev(r, x, index):
    return {"rows": r, "cols": index * NEAR_X + x}


def greet(near, nears, far, fars, r, x):
    barrier = pltpu.get_barrier_semaphore()
    for k in range(1, nears):
        pl.semaphore_signal(
            barrier, inc=1, device_id=near_dev((near + k) % nears, far), device_id_type=MESH
        )
    for k in range(1, fars):
        pl.semaphore_signal(
            barrier, inc=1, device_id=far_dev(r, x, (far + k) % fars), device_id_type=MESH
        )
    pl.semaphore_wait(barrier, nears + fars - 2)


def take_some(ref, count, sem):
    piece = ref.at[pl.ds(0, count)]
    pltpu.make_async_copy(piece, piece, sem).wait()


def moments_kernel(mode, points, rows, cols, in_ref, out_ref, near_buf, far_buf, mid, sems):
    r, x, far, fars, near, nears = group_ids(rows, cols)
    greet(near, nears, far, fars, r, x)
    for k in range(1, nears):
        pltpu.make_async_remote_copy(
            in_ref, near_buf.at[near], sems.at[0], sems.at[1],
            device_id=near_dev((near + k) % nears, far), device_id_type=MESH,
        ).start()
    near_buf[near] = in_ref[...]
    take_some(near_buf, nears - 1, sems.at[1])
    take_some(near_buf, nears - 1, sems.at[0])

    def merge(buf, count, each):
        if mode == "sum":
            return jnp.sum(buf[...], axis=0)
        half = buf.shape[1] // 2
        means = buf[:, :half]
        mean = jnp.sum(means, axis=0) * (1.0 / count)
        gap = means - mean[None]
        spread = jnp.sum(buf[:, half:], axis=0) + each * jnp.sum(gap * gap, axis=0)
        return jnp.concatenate([mean, spread], axis=0)

    mid[...] = merge(near_buf, nears, float(points))
    for k in range(1, fars):
        pltpu.make_async_remote_copy(
            mid, far_buf.at[far], sems.at[2], sems.at[3],
            device_id=far_dev(r, x, (far + k) % fars), device_id_type=MESH,
        ).start()
    far_buf[far] = mid[...]
    take_some(far_buf, fars - 1, sems.at[3])
    take_some(far_buf, fars - 1, sems.at[2])
    out_ref[...] = merge(far_buf, fars, float(points * nears))


def exchange_moments(first, second, mode, points, collective_id):
    rows, cols = lax.axis_size("rows"), lax.axis_size("cols")
    width = first.shape[0]
    lines = width // 128
    packed = jnp.concatenate([first.reshape(lines, 128), second.reshape(lines, 128)], axis=0)
    merged = pl.pallas_call(
        functools.partial(moments_kernel, mode, points, rows, cols),
        out_shape=jax.ShapeDtypeStruct(packed.shape, F32),
        in_specs=[pl.BlockSpec(memory_space=pltpu.VMEM)],
        out_specs=pl.BlockSpec(memory_space=pltpu.VMEM),
        scratch_shapes=[
            pltpu.VMEM((rows * NEAR_X,) + packed.shape, F32),
            pltpu.VMEM((cols // NEAR_X,) + packed.shape, F32),
            pltpu.VMEM(packed.shape, F32),
            pltpu.SemaphoreType.DMA((4,)),
        ],
        compiler_params=pltpu.CompilerParams(collective_id=collective_id, has_side_effects=True),
        name="moments_" + mode,
    )(packed)
    return merged[:lines].reshape(width), merged[lines:].reshape(width)


def total_kernel(rows, cols, in_ref, out_ref, near_buf, far_buf, share, piece, sems):
    r, x, far, fars, near, nears = group_ids(rows, cols)
    greet(near, nears, far, fars, r, x)
    for k in range(1, nears):
        peer = (near + k) % nears
        pltpu.make_async_remote_copy(
            in_ref.at[peer], near_buf.at[near], sems.at[0], sems.at[1],
            device_id=near_dev(peer, far), device_id_type=MESH,
        ).start()
    near_buf[near] = in_ref[near]
    take_some(near_buf, nears - 1, sems.at[1])
    share[...] = jnp.sum(near_buf[...], axis=0)
    for k in range(1, fars):
        peer = (far + k) % fars
        pltpu.make_async_remote_copy(
            share.at[peer], far_buf.at[far], sems.at[2], sems.at[3],
            device_id=far_dev(r, x, peer), device_id_type=MESH,
        ).start()
    far_buf[far] = share[far]
    take_some(far_buf, fars - 1, sems.at[3])
    piece[...] = jnp.sum(far_buf[...], axis=0)
    for k in range(1, fars):
        pltpu.make_async_remote_copy(
            piece, out_ref.at[near, far], sems.at[4], sems.at[5],
            device_id=far_dev(r, x, (far + k) % fars), device_id_type=MESH,
        ).start()
    out_ref[near, far] = piece[...]
    take_some(far_buf, fars - 1, sems.at[5])
    for k in range(1, nears):
        pltpu.make_async_remote_copy(
            out_ref.at[near], out_ref.at[near], sems.at[6], sems.at[7],
            device_id=near_dev((near + k) % nears, far), device_id_type=MESH,
        ).start()
    take_some(near_buf, nears - 1, sems.at[7])
    take_some(near_buf, nears - 1, sems.at[0])
    take_some(far_buf, fars - 1, sems.at[2])
    take_some(far_buf, fars - 1, sems.at[4])
    take_some(near_buf, nears - 1, sems.at[6])


def sum_everywhere(value, collective_id):
    rows, cols = lax.axis_size("rows"), lax.axis_size("cols")
    nears, fars = rows * NEAR_X, cols // NEAR_X
    taps, width = value.shape
    lines = -(-(taps * width) // (nears * fars * 128))
    flat = jnp.pad(value.reshape(-1, 128), ((0, nears * fars * lines - taps * width // 128), (0, 0)))
    parts = flat.reshape(nears, fars, lines, 128)
    total = pl.pallas_call(
        functools.partial(total_kernel, rows, cols),
        out_shape=jax.ShapeDtypeStruct(parts.shape, F32),
        in_specs=[pl.BlockSpec(memory_space=pltpu.VMEM)],
        out_specs=pl.BlockSpec(memory_space=pltpu.VMEM),
        scratch_shapes=[
            pltpu.VMEM((nears, fars, lines, 128), F32),
            pltpu.VMEM((fars, lines, 128), F32),
            pltpu.VMEM((fars, lines, 128), F32),
            pltpu.VMEM((lines, 128), F32),
            pltpu.SemaphoreType.DMA((8,)),
        ],
        compiler_params=pltpu.CompilerParams(collective_id=collective_id, has_side_effects=True),
        name="kernel_total",
    )(parts)
    return total.reshape(-1, 128)[: taps * width // 128].reshape(taps, width)


def rim_pixels(block, radius):
    rows, cols = lax.axis_size("rows"), lax.axis_size("cols")
    down = [(i, i + 1) for i in range(rows - 1)]
    up = [(b, a) for a, b in down]
    east = [(i, i + 1) for i in range(cols - 1)]
    west = [(b, a) for a, b in east]
    top = lax.ppermute(block[-radius:], "rows", down)
    bottom = lax.ppermute(block[:radius], "rows", up)
    channel_count = block.shape[-1]

    def strip(sel):
        return jnp.concatenate([top[:, sel], block[:, sel], bottom[:, sel]], axis=0)

    left = lax.ppermute(strip(slice(-GROUP, None)), "cols", east)
    right = lax.ppermute(strip(slice(0, GROUP)), "cols", west)
    pieces = [top, bottom, left[radius:-radius], right[radius:-radius]]
    pieces += [left[:radius], right[:radius], left[-radius:], right[-radius:]]
    return jnp.concatenate([p.reshape(-1, channel_count) for p in pieces], axis=0)


def per_device(
    features,
    dw_kernel,
    batchnorm_gain,
    batchnorm_offset,
    w_in,
    b_in,
    w_out,
    b_out,
    layer_scale,
    w_down,
    b_down,
    cotangent,
):
    tile_height, tile_width, channel_count = features.shape
    radius = (dw_kernel.shape[0] - 1) // 2
    pixel_total = tile_height * lax.axis_size("rows") * tile_width * lax.axis_size("cols")
    pixels = tile_height * tile_width
    inner_t, rim_t, tap_t, out_t, tap_o = dft_tables(tile_height, tile_width, radius)
    half = HALF
    conv_out, feat_spec, moments, out_grad = forward_part(features, cotangent, dw_kernel, w_down)
    feat_re, feat_im = feat_spec[:half], feat_spec[half:]
    area = (tile_height + 2 * radius) * (tile_width + 2 * radius)

    def pixels_of(real, imag, table):
        spec = jnp.concatenate([real, imag], axis=0).astype(jnp.bfloat16)
        return fdot(table, spec) * (1.0 / area)

    taps = jnp.pad(dw_kernel.reshape(-1, channel_count), ((0, 87), (0, 0)))
    tap_spec = fdot(tap_t, taps)
    tap_re, tap_im = tap_spec[:half], tap_spec[half:]
    lines = channel_count // 128
    mean_val = moments[:lines].reshape(channel_count)
    variance = moments[lines:].reshape(channel_count) / pixel_total
    inverse_deviation = lax.rsqrt(variance + 1e-05)
    standardized_input = (conv_out - mean_val) * inverse_deviation
    normalized_input = (
        (standardized_input * batchnorm_gain + batchnorm_offset)
        .astype(jnp.bfloat16)
    )
    pre_act = jnp.dot(normalized_input, w_in, preferred_element_type=jnp.float32) + b_in
    activated = jax.nn.gelu(pre_act).astype(jnp.bfloat16)
    branch = jnp.dot(activated, w_out, preferred_element_type=jnp.float32) + b_out
    flat_feat = features.reshape(tile_height * tile_width, channel_count).astype(jnp.float32)
    summed = (flat_feat + layer_scale * branch).astype(jnp.bfloat16)
    blocks = summed.reshape(tile_height // 2, 2, tile_width // 2, 2, channel_count)
    local_coarse = (
        jnp.einsum("paqbc,abco->opq", blocks, w_down, preferred_element_type=jnp.float32)
        + b_down[:, None, None]
    )
    coarse = lax.all_to_all(
        local_coarse.astype(jnp.bfloat16), "cols", split_axis=0, concat_axis=2, tiled=True
    )
    scaled_grad = (layer_scale * out_grad.astype(jnp.float32)).astype(jnp.bfloat16)
    act_grad = jnp.dot(scaled_grad, w_out.T, preferred_element_type=jnp.float32)
    _, pullback = jax.vjp(jax.nn.gelu, pre_act)
    pre_grad = pullback(act_grad)[0].astype(jnp.bfloat16)
    normalized_gradient = jnp.dot(pre_grad, w_in.T, preferred_element_type=jnp.float32)
    standardized_gradient = normalized_gradient * batchnorm_gain
    gradient_total, gradient_product_sum = exchange_moments(
        jnp.sum(standardized_gradient, axis=0),
        jnp.sum(standardized_gradient * standardized_input, axis=0),
        "sum", pixels, 2,
    )
    convolution_gradient = (
        inverse_deviation
        * (
            standardized_gradient
            - gradient_total / pixel_total
            - standardized_input * (gradient_product_sum / pixel_total)
        )
    ).astype(jnp.bfloat16)
    grad_inner = fdot(inner_t, convolution_gradient)
    own_re, own_im = grad_inner[:half], grad_inner[half:]
    kernel_term = pixels_of(
        feat_re * own_re + feat_im * own_im, feat_im * own_re - feat_re * own_im, tap_o[:169]
    )
    grad_kernel = sum_everywhere(kernel_term, 3) * lax.rsqrt(jnp.float32(pixel_total))
    grad_kernel = grad_kernel.reshape(dw_kernel.shape)
    rim = rim_pixels(
        convolution_gradient.reshape(tile_height, tile_width, channel_count), radius
    )
    grad_spec = grad_inner + fdot(rim_t, rim)
    grad_re, grad_im = grad_spec[:half], grad_spec[half:]
    back_conv = pixels_of(
        grad_re * tap_re - grad_im * tap_im, grad_re * tap_im + grad_im * tap_re, out_t
    )
    grad_input = (
        (out_grad.astype(jnp.float32) + back_conv)
        .astype(jnp.bfloat16)
        .reshape(tile_height, tile_width, channel_count)
    )
    return (coarse, grad_input, grad_kernel)


def solution(mesh):
    in_specs = (
        P("rows", "cols", None),
        P(),
        P(),
        P(),
        P(),
        P(),
        P(),
        P(),
        P(),
        P(),
        P(),
        P("cols", "rows", None),
    )
    out_specs = (P("cols", "rows", None), P("rows", "cols", None), P())
    return jax.shard_map(
        per_device, mesh=mesh, in_specs=in_specs, out_specs=out_specs, check_vma=False
    )
```

profile of v0, /device:TPU:24, one launch (start us, length us, event | category | flops | bytes accessed | tf_op | source)
XLA Modules:
  0.0 239.8 jit_solution(2287930505319684478)
XLA Ops:
  2.5 41.5 %forward_part.1 = (f32[1024,512]{1,0:T(8,128)}, f32[2048,512]{1,0:T(8,128)}, f32[8,128]{1,0:T(8,128)}, bf16[1024,512]{1,0:T(8,128)(2,1)}) custom-call(bf16[1024,512]{1,0:T(8,128)(2,1)} %bitcast.96, bf16[32,4,8,512]{3,2,1,0:T(8,128)(2,1)} %bitcast.97, bf16[32,16,512]{2,1,0:T(8,128)(2,1)} %cot_hbm.1, bf16[256,512]{1,0:T(8,128)(2,1)} %pad.9.tap_hbm, ...), custom_call_target="tpu_custom_call" | custom-call | tf_op jit(solution)/shard_map/forward_part/pallas_call | solution.py:408
  44.8 7.2 %fusion.30 = f32[1024,2048]{1,0:T(8,128)} fusion(bf16[512,2048]{1,0:T(8,128)(2,1)S(1)} %copy-done, f32[1024,512]{1,0:T(8,128)} %get-tuple-element.7, f32[512]{0:T(512)S(1)} %copy-done.25, f32[512]{0:T(512)S(1)} %copy-done.20, f32[512]{0:T(512)S(1)} %get-tuple-element.30, f32[512]{0:T(512)S(1)} %get-tuple-element.29), kind=kOutput, calls=%fused_computation.38 | convolution fusion | flops 2150105088 | bytes 12591104 | tf_op jit(solution)/shard_map/dot_general | solution.py:641
  52.1 14.0 %multiply_reduce_fusion.1 = (f32[512]{0:T(512)S(1)}, f32[512]{0:T(512)S(1)}, f32[1024,512]{1,0:T(8,128)}) fusion(f32[512]{0:T(512)S(1)} %copy-done.20, f32[512]{0:T(512)S(1)} %get-tuple-element.30, f32[1024,512]{1,0:T(8,128)} %get-tuple-element.7, f32[512]{0:T(512)S(1)} %get-tuple-element.29, bf16[512,2048]{1,0:T(8,128)(2,1)S(1)} %copy-done, ...), kind=kOutput, calls=%fused_computation.30 | convolution fusion | flops 4343725056 | bytes 17846272 | tf_op jit(solution)/shard_map/dot_general | solution.py:658
  66.6 15.3 %moments_sum.1 = f32[8,128]{1,0:T(8,128)} custom-call(f32[8,128]{1,0:T(8,128)} %pad_maximum_fusion.2.in_ref), custom_call_target="tpu_custom_call" | custom-call | tf_op jit(solution)/shard_map/moments_sum/pallas_call | solution.py:499
  82.8 12.9 %multiply_convert_fusion.2 = bf16[1024,512]{1,0:T(8,128)(2,1)S(1)} fusion(f32[1024,512]{1,0:T(8,128)} %get-tuple-element.31, f32[1024,512]{1,0:T(8,128)} %get-tuple-element.7, f32[512]{0:T(512)S(1)} %get-tuple-element.28, f32[512]{0:T(512)S(1)} %get-tuple-element.27, f32[512]{0:T(512)S(1)} %copy-done.20, f32[512]{0:T(512)S(1)} %get-tuple-element.30, ...), kind=kLoop, calls=%fused_computation.25 | loop fusion | flops 4194304 | bytes 5253120 | tf_op jit(solution)/shard_map/convert_element_type | solution.py:672
  98.4 3.2 %collective-permute-start = (bf16[6,32,512]{2,1,0:T(8,128)(2,1)}, bf16[6,32,512]{2,1,0:T(8,128)(2,1)}, u32[]{:S(2)}, u32[]{:S(2)}) collective-permute-start(bf16[6,32,512]{2,1,0:T(8,128)(2,1)} %bitcast.16), channel_id=1, source_target_pairs={{0,32},{32,64},{64,96},{1,33},{33,65},{65,97},{2,34},{34,66},{66,9... | collective-permute-start | bytes 589832 | tf_op jit(solution)/shard_map/ppermute | solution.py:587
  101.6 7.6 %add_convert_fusion.2 = bf16[1024,512]{1,0:T(8,128)(2,1)} fusion(bf16[1024,512]{1,0:T(8,128)(2,1)S(1)} %bitcast.98, bf16[2048,512]{1,0:T(8,128)(2,1)S(1)} %copy-done.21, f32[1024,2048]{1,0:T(8,128)} %fusion.30, f32[2048]{0:T(1024)S(1)} %copy-done.23, f32[512]{0:T(512)S(1)} %copy-done.26, f32[512]{0:T(512)S(1)} %copy-done.27), kind=kOutput, calls=%fused_computation.27 | convolution fusion | flops 2171076608 | bytes 12595200 | tf_op jit(solution)/shard_map/dot_general | solution.py:643
  110.8 3.4 %fusion.25 = bf16[1024,16,16]{0,2,1:T(8,128)(2,1)S(1)} fusion(bf16[2,2,512,1024]{3,2,1,0:T(8,128)(2,1)} %param.27, bf16[16,2,16,2,512]{4,3,2,1,0:T(2,128)(2,1)S(1)} %reshape.115, f32[1024]{0:T(1024)S(1)} %copy-done.24), kind=kOutput, calls=%fused_computation.34 | convolution fusion | flops 1074266112 | bytes 5771264 | tf_op jit(solution)/shard_map/paqbc,abco->opq/dot_general | solution.py:648
  114.2 4.7 %copy.47 = bf16[1024,16,16]{2,1,0:T(8,128)(2,1)} copy(bf16[1024,16,16]{0,2,1:T(8,128)(2,1)S(1)} %fusion.25) | data formatting | bytes 1048576 | tf_op jit(solution)/shard_map/convert_element_type | solution.py:652
  118.9 7.1 %reshape.133 = bf16[32,2,4096]{2,1,0:T(2,128)(2,1)} reshape(bf16[1024,16,16]{2,1,0:T(8,128)(2,1)} %copy.47) | data formatting | bytes 1048576
  126.0 6.6 %all-to-all-start = ((bf16[32,2,4096]{2,1,0:T(2,128)(2,1)}), bf16[32,2,4096]{2,1,0:T(2,128)(2,1)S(1)}, u32[]{:S(2)}, u32[]{:S(2)}) async-start(bf16[32,2,4096]{2,1,0:T(2,128)(2,1)} %reshape.133), calls=%async_computation | async-start | bytes 1048576 | tf_op jit(solution)/shard_map/all_to_all | solution.py:651
  132.6 2.8 %fusion.48 = f32[2048,512]{1,0:T(8,128)} fusion(bf16[2048,256]{1,0:T(8,128)(2,1)S(1)} %copy-done.6, bf16[169,512]{1,0:T(8,128)(2,1)S(1)} %reshape.113), kind=kOutput, calls=%fused_computation.62 | convolution fusion | flops 536870912 | bytes 5415936 | tf_op jit(solution)/shard_map/dot_general | solution.py:99
  142.0 27.6 %kernel_total.1 = f32[16,8,6,128]{3,2,1,0:T(8,128)} custom-call(f32[16,8,6,128]{3,2,1,0:T(8,128)} %reshape.129.in_ref), custom_call_target="tpu_custom_call" | custom-call | tf_op jit(solution)/shard_map/kernel_total/pallas_call | solution.py:563
  177.0 9.3 %collective-permute-start.3 = (bf16[44,8,512]{2,1,0:T(8,128)(2,1)}, bf16[44,8,512]{2,1,0:T(8,128)(2,1)}, u32[]{:S(2)}, u32[]{:S(2)}) collective-permute-start(bf16[44,8,512]{2,1,0:T(8,128)(2,1)} %pad_maximum_fusion.1), channel_id=1, source_target_pairs={{1,0},{2,1},{3,2},{4,3},{5,4},{6,5},{7,6},{8,7},{9,8},{10,9},{11,1... | collective-permute-start | bytes 1081352 | tf_op jit(solution)/shard_map/ppermute | solution.py:595
  186.4 3.7 %fusion.68 = f32[512,2048]{0,1:T(8,128)} fusion(bf16[2048,192]{1,0:T(8,128)(2,1)S(1)} %copy-done.12, bf16[192,512]{1,0:T(8,128)(2,1)} %bitcast.17), kind=kOutput, calls=%fused_computation.85 | convolution fusion | flops 402653184 | bytes 5177344 | tf_op jit(solution)/shard_map/dot_general | solution.py:99
  190.1 3.6 %fusion.69 = f32[512,2048]{0,1:T(8,128)} fusion(bf16[2048,192]{1,0:T(8,128)(2,1)S(1)} %copy-done.11, bf16[192,512]{1,0:T(8,128)(2,1)} %bitcast.19), kind=kOutput, calls=%fused_computation.86 | convolution fusion | flops 402653184 | bytes 5177344 | tf_op jit(solution)/shard_map/dot_general | solution.py:99
  193.7 4.1 %reshape.134 = bf16[1024,16,16]{2,1,0:T(8,128)(2,1)} reshape(bf16[32,2,4096]{2,1,0:T(2,128)(2,1)S(1)} %all-to-all-done) | data formatting | bytes 1048576
  197.8 4.6 %copy.48 = bf16[32,32,16,16]{1,3,0,2:T(8,128)(2,1)S(1)} copy(bf16[32,32,16,16]{3,2,1,0:T(8,128)(2,1)} %bitcast.93) | data formatting | bytes 1048576 | tf_op jit(solution)/shard_map/all_to_all | solution.py:651
  204.2 3.6 %fusion.46 = f32[512,2048]{0,1:T(8,128)} fusion(bf16[2048,48]{1,0:T(8,128)(2,1)} %constant.57, bf16[44,8,512]{2,1,0:T(8,128)(2,1)} %collective-permute-done.3), kind=kOutput, calls=%fused_computation.59 | convolution fusion | flops 100663296 | bytes 4767744 | tf_op jit(solution)/shard_map/dot_general | solution.py:99
  209.6 2.7 %fusion.45 = f32[512,2048]{0,1:T(8,128)} fusion(bf16[2048,48]{1,0:T(8,128)(2,1)S(1)} %copy-done.17, bf16[44,8,512]{2,1,0:T(8,128)(2,1)S(1)} %collective-permute-done.2), kind=kOutput, calls=%fused_computation.57 | convolution fusion | flops 100663296 | bytes 4767744 | tf_op jit(solution)/shard_map/dot_general | solution.py:99
  212.3 2.7 %fusion.47 = f32[512,2048]{0,1:T(8,128)} fusion(bf16[2048,48]{1,0:T(8,128)(2,1)S(1)} %copy-done.16, bf16[44,8,512]{2,1,0:T(8,128)(2,1)S(1)} %collective-permute-done.2), kind=kOutput, calls=%fused_computation.61 | convolution fusion | flops 100663296 | bytes 4767744 | tf_op jit(solution)/shard_map/dot_general | solution.py:99
  218.5 10.4 %bitcast_add_fusion = f32[2048,512]{1,0:T(8,128)} fusion(f32[2048,512]{1,0:T(8,128)} %copy-done.4, f32[512,2048]{0,1:T(8,128)} %fusion.45, f32[512,2048]{0,1:T(8,128)} %fusion.46, f32[512,2048]{0,1:T(8,128)} %fusion.47, f32[512,2048]{0,1:T(8,128)S(1)} %fusion.42, f32[512,2048]{0,1:T(8,128)S(1)} %fusion.43, f32[512,2048]{0,1:T(8,128)S(1)} %copy-done.2, ...), kind=kOutput, calls=%fused_computation.10 | convolution fusion | flops 109051904 | bytes 37994496 | tf_op jit(solution)/shard_map/dot_general | solution.py:99
  228.9 5.5 %fusion.40 = f32[512,1024]{0,1:T(8,128)S(1)} fusion(bf16[1024,1024]{1,0:T(8,128)(2,1)} %constant.60, f32[2048,512]{1,0:T(8,128)} %fusion.48, f32[2048,512]{1,0:T(8,128)} %bitcast_add_fusion), kind=kOutput, calls=%fused_computation.45 | convolution fusion | flops 1075838976 | bytes 12582912 | tf_op jit(solution)/shard_map/dot_general | solution.py:99
  235.6 3.9 %fusion.15 = bf16[1024,512]{1,0:T(8,128)(2,1)} fusion(bf16[1024,512]{1,0:T(8,128)(2,1)S(1)} %copy-done.22, f32[512,1024]{0,1:T(8,128)S(1)} %fusion.40, bf16[1024,1024]{1,0:T(8,128)(2,1)} %constant.61, f32[2048,512]{1,0:T(8,128)S(1)} %copy-done.5, f32[2048,512]{1,0:T(8,128)S(1)} %copy-done.7), kind=kOutput, calls=%fused_computation.19 | convolution fusion | flops 1078460416 | bytes 14680064 | tf_op jit(solution)/shard_map/dot_general | solution.py:99
  (87 shorter events, 30.5 us)
Async XLA Ops:
  0.6 44.1 %copy-start = (bf16[512,2048]{1,0:T(8,128)(2,1)S(1)}, bf16[512,2048]{1,0:T(8,128)(2,1)}, u32[]{:S(2)}) copy-start(bf16[512,2048]{1,0:T(8,128)(2,1)} %param.22) | copy-start | bytes 6291460
  2.5 42.3 %copy-start.20 = (f32[512]{0:T(512)S(1)}, f32[512]{0:T(512)}, u32[]{:S(2)}) copy-start(f32[512]{0:T(512)} %param.20) | copy-start | bytes 6148
  2.5 42.3 %copy-start.25 = (f32[512]{0:T(512)S(1)}, f32[512]{0:T(512)}, u32[]{:S(2)}) copy-start(f32[512]{0:T(512)} %param.21) | copy-start | bytes 6148
  44.8 7.3 %copy-start.23 = (f32[2048]{0:T(1024)S(1)}, f32[2048]{0:T(1024)}, u32[]{:S(2)}) copy-start(f32[2048]{0:T(1024)} %param.23) | copy-start | bytes 24580
  44.8 7.3 %copy-start.27 = (f32[512]{0:T(512)S(1)}, f32[512]{0:T(512)}, u32[]{:S(2)}) copy-start(f32[512]{0:T(512)} %param.26) | copy-start | bytes 6148
  66.0 35.6 %copy-start.10 = (bf16[32,32,512]{2,1,0:T(8,128)(2,1)S(1)}, bf16[32,32,512]{2,1,0:T(8,128)(2,1)}, u32[]{:S(2)}) copy-start(bf16[32,32,512]{2,1,0:T(8,128)(2,1)} %param.18) | copy-start | bytes 3145732
  66.0 35.6 %copy-start.26 = (f32[512]{0:T(512)S(1)}, f32[512]{0:T(512)}, u32[]{:S(2)}) copy-start(f32[512]{0:T(512)} %param.25) | copy-start | bytes 6148
  81.9 19.7 %copy-start.21 = (bf16[2048,512]{1,0:T(8,128)(2,1)S(1)}, bf16[2048,512]{1,0:T(8,128)(2,1)}, u32[]{:S(2)}) copy-start(bf16[2048,512]{1,0:T(8,128)(2,1)} %param.24) | copy-start | bytes 6291460
  96.5 75.1 %collective-permute-start.1 = (bf16[6,32,512]{2,1,0:T(8,128)(2,1)}, bf16[6,32,512]{2,1,0:T(8,128)(2,1)}, u32[]{:S(2)}, u32[]{:S(2)}) collective-permute-start(bf16[6,32,512]{2,1,0:T(8,128)(2,1)} %bitcast.18), channel_id=1, source_target_pairs={{32,0},{64,32},{96,64},{33,1},{65,33},{97,65},{34,2},{66,34},{98,6... | collective-permute-start | bytes 589832 | tf_op jit(solution)/shard_map/ppermute | solution.py:588
  98.4 12.4 %copy-start.24 = (f32[1024]{0:T(1024)S(1)}, f32[1024]{0:T(1024)}, u32[]{:S(2)}) copy-start(f32[1024]{0:T(1024)} %param.28) | copy-start | bytes 12292
  98.4 74.0 %collective-permute-start = (bf16[6,32,512]{2,1,0:T(8,128)(2,1)}, bf16[6,32,512]{2,1,0:T(8,128)(2,1)}, u32[]{:S(2)}, u32[]{:S(2)}) collective-permute-start(bf16[6,32,512]{2,1,0:T(8,128)(2,1)} %bitcast.16), channel_id=1, source_target_pairs={{0,32},{32,64},{64,96},{1,33},{33,65},{65,97},{2,34},{34,66},{66,9... | collective-permute-start | bytes 589832 | tf_op jit(solution)/shard_map/ppermute | solution.py:587
  114.2 18.4 %copy-start.6 = (bf16[2048,256]{1,0:T(8,128)(2,1)S(1)}, bf16[2048,256]{1,0:T(8,128)(2,1)}, u32[]{:S(2)}) copy-start(bf16[2048,256]{1,0:T(8,128)(2,1)} %constant.44.clone.ftap_hbm) | copy-start | bytes 3145732
  126.0 67.7 %all-to-all-start = ((bf16[32,2,4096]{2,1,0:T(2,128)(2,1)}), bf16[32,2,4096]{2,1,0:T(2,128)(2,1)S(1)}, u32[]{:S(2)}, u32[]{:S(2)}) async-start(bf16[32,2,4096]{2,1,0:T(2,128)(2,1)} %reshape.133), calls=%async_computation | async-start | bytes 1048576 | tf_op jit(solution)/shard_map/all_to_all | solution.py:651
  132.6 3.5 %copy-start.9 = (bf16[2048,1024]{1,0:T(8,128)(2,1)S(1)}, bf16[2048,1024]{1,0:T(8,128)(2,1)}, u32[]{:S(2)}) copy-start(bf16[2048,1024]{1,0:T(8,128)(2,1)} %constant.42.clone.fin_hbm) | copy-start | bytes 12582916
  141.0 45.3 %copy-start.12 = (bf16[2048,192]{1,0:T(8,128)(2,1)S(1)}, bf16[2048,192]{1,0:T(8,128)(2,1)}, u32[]{:S(2)}) copy-start(bf16[2048,192]{1,0:T(8,128)(2,1)} %constant.52) | copy-start | bytes 2359300
  174.0 35.6 %collective-permute-start.2 = (bf16[44,8,512]{2,1,0:T(8,128)(2,1)}, bf16[44,8,512]{2,1,0:T(8,128)(2,1)S(1)}, u32[]{:S(2)}, u32[]{:S(2)}) collective-permute-start(bf16[44,8,512]{2,1,0:T(8,128)(2,1)} %pad_maximum_fusion), channel_id=1, source_target_pairs={{0,1},{1,2},{2,3},{3,4},{4,5},{5,6},{6,7},{7,8},{8,9},{9,10},{10,1... | collective-permute-start | bytes 1081352 | tf_op jit(solution)/shard_map/ppermute | solution.py:594
  177.0 27.2 %collective-permute-start.3 = (bf16[44,8,512]{2,1,0:T(8,128)(2,1)}, bf16[44,8,512]{2,1,0:T(8,128)(2,1)}, u32[]{:S(2)}, u32[]{:S(2)}) collective-permute-start(bf16[44,8,512]{2,1,0:T(8,128)(2,1)} %pad_maximum_fusion.1), channel_id=1, source_target_pairs={{1,0},{2,1},{3,2},{4,3},{5,4},{6,5},{7,6},{8,7},{9,8},{10,9},{11,1... | collective-permute-start | bytes 1081352 | tf_op jit(solution)/shard_map/ppermute | solution.py:595
  186.4 3.7 %copy-start.11 = (bf16[2048,192]{1,0:T(8,128)(2,1)S(1)}, bf16[2048,192]{1,0:T(8,128)(2,1)}, u32[]{:S(2)}) copy-start(bf16[2048,192]{1,0:T(8,128)(2,1)} %constant.53) | copy-start | bytes 2359300
  202.4 5.5 %copy-start.14 = (bf16[2048,256]{1,0:T(8,128)(2,1)S(1)}, bf16[2048,256]{1,0:T(8,128)(2,1)}, u32[]{:S(2)}) copy-start(bf16[2048,256]{1,0:T(8,128)(2,1)} %constant.55) | copy-start | bytes 3145732
  209.5 5.4 %copy-start.13 = (bf16[2048,256]{1,0:T(8,128)(2,1)S(1)}, bf16[2048,256]{1,0:T(8,128)(2,1)}, u32[]{:S(2)}) copy-start(bf16[2048,256]{1,0:T(8,128)(2,1)} %constant.54) | copy-start | bytes 3145732
  228.9 5.5 %copy-start.5 = (f32[2048,512]{1,0:T(8,128)S(1)}, f32[2048,512]{1,0:T(8,128)}, u32[]{:S(2)}) copy-start(f32[2048,512]{1,0:T(8,128)} %fusion.48) | copy-start | bytes 12582916
  228.9 6.5 %copy-start.7 = (f32[2048,512]{1,0:T(8,128)S(1)}, f32[2048,512]{1,0:T(8,128)}, u32[]{:S(2)}) copy-start(f32[2048,512]{1,0:T(8,128)} %bitcast_add_fusion) | copy-start | bytes 12582916
  228.9 6.7 %copy-start.22 = (bf16[1024,512]{1,0:T(8,128)(2,1)S(1)}, bf16[1024,512]{1,0:T(8,128)(2,1)}, u32[]{:S(2)}) copy-start(bf16[1024,512]{1,0:T(8,128)(2,1)} %get-tuple-element.9) | copy-start | bytes 3145732
  228.9 10.7 %copy-start.1 = (bf16[512,2048]{1,0:T(8,128)(2,1)S(1)}, bf16[512,2048]{1,0:T(8,128)(2,1)}, u32[]{:S(2)}) copy-start(bf16[512,2048]{1,0:T(8,128)(2,1)} %param.22) | copy-start | bytes 6291460
  (9 other events, 22.4 us)
where the time goes:
time: 244 us; the launch traced here: 240 us
  Pallas kernels  84.3 us (35%)
  matrix products  77.1 us (32%)
  local copies, waits for them, and re-layouts  37.1 us (15%)
  starting transfers between devices  23.2 us (10%)
  other arithmetic  16.7 us (7%)
    dot_general x14, matrix products, fdot(): return jnp.dot(a, b, preferred_element_type=F32)  44.8 us
    pallas_call x1, Pallas kernels, forward_part(): pl.pallas_call(functools.partial(forward_kernel, rows, cols, radius), out...  41.5 us
    pallas_call x1, Pallas kernels, sum_everywhere(): pl.pallas_call(functools.partial(total_kernel, rows, cols), out_shape=jax...  27.6 us
    unnamed x59, local copies, waits for them, and re-layouts  19.2 us
    pallas_call x1, Pallas kernels, exchange_moments(): pl.pallas_call(functools.partial(moments_kernel, mode, points, rows, cols...  15.3 us
    dot_general x1, matrix products, per_device(): jnp.dot(pre_grad, w_in.T, preferred_element_type=jnp.float32)  14 us
    convert_element_type x1, other arithmetic, per_device(): convolution_gradient = (inverse_deviation * (standardized_gradient - grad...  12.9 us
    ppermute x1, starting transfers between devices, rim_pixels(): right = lax.ppermute(strip(slice(0, GROUP)), 'cols', west)  9.34 us
  transfers between devices with their start and end apart: 5, of which 0 were waited for; matrix products, arithmetic and copies ran while one was open for 25% of the time, Pallas kernels for 11%

commit v1 on v0

v1 whole, which is shorter than its diff:
```python
import functools

import jax
import jax.numpy as jnp
import numpy as np
from jax import lax
from jax.experimental import pallas as pl
from jax.experimental.pallas import tpu as pltpu
from jax.sharding import PartitionSpec as P

MESH = pl.DeviceIdType.MESH
F32 = jnp.float32
BF16 = jnp.bfloat16
NEAR_X = 4
GROUP = 8
HALF = 1024
TAP_LINE = 16
TAP_TILES = 7
TAP_ROWS = 4 * TAP_TILES * 8
GELU_A, GELU_B = 0.7978845608028654, 0.044715
CHUNK = 256


def balanced(table):
    low = table.astype(jnp.bfloat16)
    bits = low.view(np.uint16)
    up = (bits + 1).astype(np.uint16).view(jnp.bfloat16).astype(np.float64)
    down = (bits - 1).astype(np.uint16).view(jnp.bfloat16).astype(np.float64)
    value = low.astype(np.float64)
    out = value.copy()
    for row in range(table.shape[0]):
        excess = (value[row] - table[row]).sum()
        if excess == 0.0:
            continue
        live = np.nonzero(np.abs(table[row]) > 0.004)[0]
        steps = np.stack([up[row, live], down[row, live]]) - value[row, live]
        order = np.argsort(-np.abs(steps[0]), kind="stable")
        for spot in order:
            for step in steps[:, spot]:
                if abs(excess + step) < abs(excess) - 0.25 * abs(step):
                    out[row, live[spot]] += step
                    excess += step
                    break
    return out.astype(jnp.bfloat16)


@functools.lru_cache(maxsize=None)
def dft_tables(tile_h, tile_w, radius):
    nh, nw = tile_h + 2 * radius, tile_w + 2 * radius
    u, v, weight = np.zeros(HALF), np.zeros(HALF), np.zeros(HALF)
    index = 0
    for a in range(nh):
        for b in range(nw // 2 + 1):
            edge = b in (0, nw // 2)
            if edge and a > nh // 2:
                continue
            u[index], v[index] = a, b
            weight[index] = 1.0 if edge and a in (0, nh // 2) else 2.0
            index += 1
    live = weight > 0

    def rows(points):
        p = np.asarray(points)
        turns = (np.outer(u, p[:, 0]) % nh) / nh + (np.outer(v, p[:, 1]) % nw) / nw
        angle = 2.0 * np.pi * turns
        table = np.concatenate([np.cos(angle) * live[:, None], -np.sin(angle) * live[:, None]])
        table[np.abs(table) < 1e-9] = 0.0
        return table

    inner = [(h, w) for h in range(tile_h) for w in range(tile_w)]
    wests = range(-GROUP, 0)
    easts = range(tile_w, tile_w + GROUP)
    norths = range(-radius, 0)
    souths = range(tile_h, tile_h + radius)
    rim = [(h, w) for hs in (norths, souths) for h in hs for w in range(tile_w)]
    rim += [(h, w) for ws in (wests, easts) for h in range(tile_h) for w in ws]
    rim += [(h, w) for hs in (norths, souths) for ws in (wests, easts) for h in hs for w in ws]
    kept = np.asarray([-radius <= w < tile_w + radius for _, w in rim])
    taps = [(i, j) for i in range(-radius, radius + 1) for j in range(-radius, radius + 1)]
    both = balanced(np.concatenate([rows(inner), rows(rim) * kept[None]], axis=1))
    count = len(inner)
    spot = [(i + radius) * TAP_LINE + j + radius for i, j in taps]
    doubled = np.concatenate([weight, weight])[None]
    f_tap = np.zeros((2 * HALF, CHUNK))
    f_tap[:, spot] = rows(taps)
    g_tap = np.zeros((TAP_ROWS, 2 * HALF))
    g_tap[spot] = rows(taps).T * doubled
    f_tap, g_tap = f_tap.astype(jnp.bfloat16), g_tap.astype(jnp.bfloat16)
    f_out = (rows(inner).T * doubled).astype(jnp.bfloat16)
    return both[:, :count], both[:, count:], f_tap, f_out, g_tap


@functools.lru_cache(maxsize=None)
def phase_table(tile_w):
    table = np.zeros((CHUNK, CHUNK), np.float32)
    lines = CHUNK // tile_w
    for h in range(lines):
        for w in range(tile_w):
            plane = (h % 2) * 2 + w % 2
            table[plane * 64 + (h // 2) * (tile_w // 2) + w // 2, h * tile_w + w] = 1.0
    return table.astype(jnp.bfloat16)


def fdot(a, b):
    return jnp.dot(a, b, preferred_element_type=F32)


def ndot(a, b):
    return lax.dot_general(a, b, (((1,), (1,)), ((), ())), preferred_element_type=F32)


def rows_of(step, size=CHUNK):
    return pl.ds(pl.multiple_of(step * size, size), size)


def swap_blocks(parts):
    lane = lax.broadcasted_iota(jnp.int32, parts[0].shape, 1) // 16
    parts = list(parts)
    for k in (1, 2, 4):
        low = (lane // k) % 2 == 0
        for i in range(8):
            if i & k:
                continue
            a, b = parts[i], parts[i | k]
            parts[i] = jnp.where(low, a, pltpu.roll(b, 16 * k, 1))
            parts[i | k] = jnp.where(low, pltpu.roll(a, 128 - 16 * k, 1), b)
    return parts


class Place:
    def __init__(self, rows, cols):
        self.rows, self.cols = rows, cols
        self.r, self.c = lax.axis_index("rows"), lax.axis_index("cols")
        self.x, self.far = self.c % NEAR_X, self.c // NEAR_X
        self.fars, self.nears = cols // NEAR_X, rows * NEAR_X
        self.near = self.r * NEAR_X + self.x

    def near_dev(self, k):
        peer = (self.near + k) % self.nears
        return peer, {"rows": peer // NEAR_X, "cols": self.far * NEAR_X + peer % NEAR_X}

    def far_dev(self, k):
        peer = (self.far + k) % self.fars
        return peer, {"rows": self.r, "cols": peer * NEAR_X + self.x}

    def col_dev(self, k):
        peer = (self.c + k) % self.cols
        return peer, {"rows": self.r, "cols": peer}

    def inside(self, dr, dc):
        r, c = self.r + dr, self.c + dc
        return (r >= 0) & (r < self.rows) & (c >= 0) & (c < self.cols)

    def rim_dev(self, dr, dc):
        return {"rows": self.r + dr, "cols": self.c + dc}

    def greet(self):
        barrier = pltpu.get_barrier_semaphore()
        for dr, dc in STEPS:
            @pl.when(self.inside(dr, dc))
            def _():
                pl.semaphore_signal(
                    barrier, inc=1, device_id=self.rim_dev(dr, dc), device_id_type=MESH
                )
        for count, dev in (
            (self.nears, self.near_dev), (self.fars, self.far_dev), (self.cols, self.col_dev)
        ):
            for k in range(1, count):
                pl.semaphore_signal(barrier, inc=1, device_id=dev(k)[1], device_id_type=MESH)

    def met(self):
        def beside(at, size):
            return 1 + (at + size - 1) // size + (2 * size - 2 - at) // size

        around = beside(self.r, self.rows) * beside(self.c, self.cols) - 1
        pl.semaphore_wait(
            pltpu.get_barrier_semaphore(), around + self.nears + self.fars + self.cols - 3
        )


STEPS = ((1, 0), (-1, 0), (0, 1), (0, -1), (1, 1), (1, -1), (-1, 1), (-1, -1))


def send(src, dst, sems, slot, dev):
    pltpu.make_async_remote_copy(
        src, dst, sems.at[slot], sems.at[slot + 1], device_id=dev, device_id_type=MESH
    ).start()


def take(ref, sem):
    pltpu.make_async_copy(ref, ref, sem).wait()


def rim_pieces(block, radius, tb, lr, corner):
    lines, groups = block.shape[0], block.shape[1]
    south, north = pl.ds(lines - radius, radius), pl.ds(0, radius)
    last = groups - 1
    return (
        (block.at[south], tb.at[0]),
        (block.at[north], tb.at[1]),
        (block.at[:, last], lr.at[0]),
        (block.at[:, 0], lr.at[1]),
        (block.at[south, last], corner.at[0]),
        (block.at[south, 0], corner.at[1]),
        (block.at[north, last], corner.at[2]),
        (block.at[north, 0], corner.at[3]),
    )


def start_rim(place, pieces, sems):
    for (dr, dc), (src, dst), k in zip(STEPS, pieces, range(8)):
        @pl.when(place.inside(dr, dc))
        def _():
            send(src, dst, sems, 2 * k, place.rim_dev(dr, dc))


def finish_rim(place, pieces, sems, tb, lr, corner, rim):
    for (dr, dc), (_, dst), k in zip(STEPS, pieces, range(8)):
        @pl.when(place.inside(-dr, -dc))
        def _():
            take(dst, sems.at[2 * k + 1])

        @pl.when(jnp.logical_not(place.inside(-dr, -dc)))
        def _():
            dst[...] = jnp.zeros(dst.shape, BF16)

    channels = rim.shape[1]
    at = 0
    for ref in (tb, lr, corner):
        count = int(np.prod(ref.shape[:-1]))
        flat = ref[...].astype(F32).reshape(count, channels).astype(BF16)
        rim[at : at + count] = flat
        at += count


def drain_rim(place, pieces, sems):
    for (dr, dc), (_, dst), k in zip(STEPS, pieces, range(8)):
        @pl.when(place.inside(dr, dc))
        def _():
            take(dst, sems.at[2 * k])


def lines_of(row):
    return jnp.concatenate([row[:, k * 128 : (k + 1) * 128] for k in range(row.shape[1] // 128)], 0)


def row_of(lines):
    return jnp.concatenate([lines[k : k + 1] for k in range(lines.shape[0])], 1)


def merge_moments(buf, count, each):
    half = buf.shape[1] // 2
    means = buf[:, :half]
    mean = jnp.sum(means, axis=0) * (1.0 / count)
    gap = means - mean[None]
    spread = jnp.sum(buf[:, half:], axis=0) + each * jnp.sum(gap * gap, axis=0)
    return jnp.concatenate([mean, spread], axis=0)


def step_kernel(
    rows, cols, radius,
    feat_hbm, feat4_hbm, cot_hbm, tap_hbm, fin_hbm, frim_hbm, ftap_hbm, fout_hbm, gtap_hbm,
    down_hbm, phase_hbm, win_hbm, wout_hbm, gain, offset, b_in, b_out, scale, b_down,
    coarse_ref, grad_in_ref, grad_tap_ref,
    feat, cot, tap_raw, fin, frim, ftap, fout, gtap, down, phase, win, wout,
    cot32, spread, cot_in, coarse_in, taps, tap_spec, mixed, spec, own, conv, grad, xgrad, act,
    tb, lr, corner, rim, planes, edge,
    near_buf, far_buf, near_sum, far_sum, mine, mid, sums, sums_mid,
    tap_part, tap_near, tap_share, tap_far, tap_piece, tap_all,
    in_sems, rim_sems, sems,
):
    place = Place(rows, cols)
    sources = (
        (cot_hbm, cot), (tap_hbm, tap_raw), (ftap_hbm, ftap), (feat_hbm, feat), (fin_hbm, fin),
        (frim_hbm, frim), (fout_hbm, fout), (down_hbm, down), (phase_hbm, phase),
        (win_hbm, win), (wout_hbm, wout), (gtap_hbm, gtap),
    )
    loads = [
        pltpu.make_async_copy(src, dst, in_sems.at[k]) for k, (src, dst) in enumerate(sources)
    ]
    for load in loads:
        load.start()
    place.greet()

    outs, lines, width = cot.shape
    pixels, channels = conv.shape
    side = pixels // (2 * lines)
    parts_n = pixels // CHUNK
    area = (2 * lines + 2 * radius) * (side + 2 * radius)
    everything = float(pixels * rows * cols)
    zero = jnp.zeros((1, channels), F32)

    loads[0].wait()
    for tg in range(width // 128):
        cot32[tg] = cot[:, :, tg * 128 : (tg + 1) * 128].astype(F32).reshape(outs * lines, 128)
        for pg in range(lines // 8):
            parts = swap_blocks([
                cot32[tg, pl.ds(pg * 8 + k, outs, stride=lines), :] for k in range(8)
            ])
            for k in range(8):
                spread[tg * 8 + k, :, pg * 128 : (pg + 1) * 128] = parts[k].astype(BF16)
    place.met()
    pieces = rim_pieces(feat4_hbm, radius, tb, lr, corner)
    start_rim(place, pieces, rim_sems)
    for k in range(1, cols):
        peer, dev = place.col_dev(k)
        send(spread.at[peer], cot_in.at[place.c], sems, 0, dev)
    cot_in[place.c] = spread[place.c]

    loads[1].wait()
    loads[2].wait()
    taps[...] = jnp.zeros(taps.shape, BF16)
    for i in range(2 * radius + 1):
        taps[i * TAP_LINE : i * TAP_LINE + 2 * radius + 1] = tap_raw[i]

    @pl.loop(0, 2 * HALF // CHUNK)
    def _(m):
        tap_spec[rows_of(m)] = fdot(ftap[rows_of(m)], taps[...])

    loads[3].wait()
    loads[4].wait()

    @pl.loop(0, 2 * HALF // CHUNK)
    def _(m):
        spec[rows_of(m)] = fdot(fin[rows_of(m)], feat[...])

    finish_rim(place, pieces, rim_sems, tb, lr, corner, rim)
    loads[5].wait()

    @pl.loop(0, HALF // CHUNK)
    def _(m):
        re, im = rows_of(m), rows_of(m + HALF // CHUNK)
        fr = spec[re] + fdot(frim[re], rim[...])
        fi = spec[im] + fdot(frim[im], rim[...])
        spec[re], spec[im] = fr, fi
        kr, ki = tap_spec[re], tap_spec[im]
        mixed[re] = (fr * kr + fi * ki).astype(BF16)
        mixed[im] = (fi * kr - fr * ki).astype(BF16)

    loads[6].wait()

    def invert(m, total):
        block = fdot(fout[rows_of(m)], mixed[...]) * (1.0 / area)
        conv[rows_of(m)] = block
        return total + jnp.sum(block, axis=0, keepdims=True)

    local = lax.fori_loop(0, parts_n, invert, zero) * (1.0 / pixels)

    def scatter(m, total):
        gap = conv[rows_of(m)] - local
        return total + jnp.sum(gap * gap, axis=0, keepdims=True)

    around = lax.fori_loop(0, parts_n, scatter, zero)
    mine[...] = jnp.concatenate([lines_of(local), lines_of(around)], axis=0)
    for k in range(1, place.nears):
        send(mine, near_buf.at[place.near], sems, 2, place.near_dev(k)[1])
    near_buf[place.near] = mine[...]

    take(cot_in.at[pl.ds(0, cols - 1)], sems.at[1])
    loads[7].wait()
    loads[8].wait()
    tall = cot_in[...].reshape(cols * outs, lines * lines).astype(F32).T.astype(BF16)
    for ab in range(4):
        planes[ab] = ndot(tall, down[ab]).astype(BF16)
    take(near_buf.at[pl.ds(0, place.nears - 1)], sems.at[3])
    mid[...] = merge_moments(near_buf, place.nears, float(pixels))
    for k in range(1, place.fars):
        send(mid, far_buf.at[place.far], sems, 4, place.far_dev(k)[1])
    far_buf[place.far] = mid[...]
    for k in range(parts_n):
        block = jnp.concatenate([planes[ab, k * 64 : (k + 1) * 64] for ab in range(4)], axis=0)
        grad[k * CHUNK : (k + 1) * CHUNK] = lax.dot_general(
            phase[...], block, (((0,), (0,)), ((), ())), preferred_element_type=F32
        ).astype(BF16)
    take(far_buf.at[pl.ds(0, place.fars - 1)], sems.at[5])
    moments = merge_moments(far_buf, place.fars, float(pixels * place.nears))
    take(cot_in.at[pl.ds(0, cols - 1)], sems.at[0])
    drain_rim(place, pieces, rim_sems)

    half = moments.shape[0] // 2
    mean = row_of(moments[:half])
    inverse = lax.rsqrt(row_of(moments[half:]) * (1.0 / everything) + 1e-05)
    loads[9].wait()
    loads[10].wait()
    hidden = win.shape[1]
    step = 512

    def mlp(m, totals):
        at = rows_of(m)
        xhat = (conv[at] - mean) * inverse
        normed = (xhat * gain[...] + offset[...]).astype(BF16)
        scaled = (scale[...] * grad[at].astype(F32)).astype(BF16)
        back = jnp.zeros((CHUNK, channels), F32)
        for j in range(hidden // step):
            cut = slice(j * step, (j + 1) * step)
            v = fdot(normed, win[:, cut]) + b_in[:, cut]
            act_grad = ndot(scaled, wout[cut])
            square = v * v
            t = jnp.tanh(GELU_A * v * (1.0 + GELU_B * square))
            gate = 0.5 * (1.0 + t)
            act[at, cut] = (v * gate).astype(BF16)
            slope = gate + (0.5 * GELU_A) * v * (1.0 - t * t) * (1.0 + (3.0 * GELU_B) * square)
            back = back + ndot((act_grad * slope).astype(BF16), win[:, cut])
        back = back * gain[...]
        xgrad[at] = back
        return (
            totals[0] + jnp.sum(back, axis=0, keepdims=True),
            totals[1] + jnp.sum(back * xhat, axis=0, keepdims=True),
        )

    total, product = lax.fori_loop(0, parts_n, mlp, (zero, zero))
    sums[...] = jnp.concatenate([lines_of(total), lines_of(product)], axis=0)
    for k in range(1, place.nears):
        send(sums, near_sum.at[place.near], sems, 6, place.near_dev(k)[1])
    near_sum[place.near] = sums[...]

    for k in range(parts_n):
        at = slice(k * CHUNK, (k + 1) * CHUNK)
        branch = fdot(act[at], wout[...]) + b_out[...]
        summed = (feat[at].astype(F32) + scale[...] * branch).astype(BF16)
        split = fdot(phase[...], summed).astype(BF16)
        for ab in range(4):
            planes[ab, k * 64 : (k + 1) * 64] = split[ab * 64 : (ab + 1) * 64]
    take(near_sum.at[pl.ds(0, place.nears - 1)], sems.at[7])
    sums_mid[...] = jnp.sum(near_sum[...], axis=0)
    for k in range(1, place.fars):
        send(sums_mid, far_sum.at[place.far], sems, 8, place.far_dev(k)[1])
    far_sum[place.far] = sums_mid[...]
    flat = b_down[...]
    for ab in range(4):
        flat = flat + fdot(planes[ab], down[ab])
    spread[...] = flat.T.astype(BF16).reshape(cols, outs, lines * lines)
    for k in range(1, cols):
        peer, dev = place.col_dev(k)
        send(spread.at[peer], coarse_in.at[place.c], sems, 10, dev)
    coarse_in[place.c] = spread[place.c]
    take(far_sum.at[pl.ds(0, place.fars - 1)], sems.at[9])
    both = jnp.sum(far_sum[...], axis=0) * (1.0 / everything)
    level, slant = row_of(both[:half]), row_of(both[half:])

    groups = edge.shape[1]
    for k in range(parts_n):
        at = slice(k * CHUNK, (k + 1) * CHUNK)
        xhat = (conv[at] - mean) * inverse
        block = inverse * (xgrad[at] - level - xhat * slant)
        feat[at] = block.astype(BF16)
        tall_lines = CHUNK // side
        edge[k * tall_lines : (k + 1) * tall_lines] = block.reshape(
            tall_lines, groups, GROUP, channels
        ).astype(BF16)
    pieces = rim_pieces(edge, radius, tb, lr, corner)
    start_rim(place, pieces, rim_sems)

    @pl.loop(0, HALF // CHUNK)
    def _(m):
        re, im = rows_of(m), rows_of(m + HALF // CHUNK)
        gr, gi = fdot(fin[re], feat[...]), fdot(fin[im], feat[...])
        own[re], own[im] = gr, gi
        fr, fi = spec[re], spec[im]
        mixed[re] = (fr * gr + fi * gi).astype(BF16)
        mixed[im] = (fi * gr - fr * gi).astype(BF16)

    loads[11].wait()
    norm = 1.0 / (area * float(np.sqrt(everything)))
    tap_part[...] = (fdot(gtap[...], mixed[...]) * norm).reshape(tap_part.shape)

    def tap_block(index):
        start = pl.multiple_of((index % NEAR_X) * 128, 128)
        return tap_part.at[pl.ds((index // NEAR_X) * TAP_TILES, TAP_TILES), :, pl.ds(start, 128)]

    for k in range(1, place.nears):
        peer, dev = place.near_dev(k)
        send(tap_block(peer), tap_near.at[place.near], sems, 12, dev)
    tap_near[place.near] = tap_block(place.near)[...]

    finish_rim(place, pieces, rim_sems, tb, lr, corner, rim)

    @pl.loop(0, HALF // CHUNK)
    def _(m):
        re, im = rows_of(m), rows_of(m + HALF // CHUNK)
        gr = own[re] + fdot(frim[re], rim[...])
        gi = own[im] + fdot(frim[im], rim[...])
        kr, ki = tap_spec[re], tap_spec[im]
        mixed[re] = (gr * kr - gi * ki).astype(BF16)
        mixed[im] = (gr * ki + gi * kr).astype(BF16)

    take(tap_near.at[pl.ds(0, place.nears - 1)], sems.at[13])
    tap_share[...] = jnp.sum(tap_near[...], axis=0)
    owner = place.far < TAP_TILES
    for k in range(1, place.fars):
        peer, dev = place.far_dev(k)

        @pl.when(peer < TAP_TILES)
        def _():
            send(tap_share.at[peer], tap_far.at[place.far], sems, 14, dev)

    def spread_out(m):
        at = slice(m * CHUNK, (m + 1) * CHUNK)
        block = fdot(fout[at], mixed[...]) * (1.0 / area)
        grad_in_ref[at] = (grad[at].astype(F32) + block).astype(BF16)

    for m in range(parts_n // 2):
        spread_out(m)

    @pl.when(owner)
    def _():
        tap_far[place.far] = tap_share[place.far]
        take(tap_far.at[pl.ds(0, place.fars - 1)], sems.at[15])
        tap_piece[...] = jnp.sum(tap_far[...], axis=0)
        for k in range(1, place.fars):
            send(tap_piece, tap_all.at[place.near, place.far], sems, 16, place.far_dev(k)[1])
        tap_all[place.near, place.far] = tap_piece[...]

    for m in range(parts_n // 2, parts_n):
        spread_out(m)

    @pl.when(owner)
    def _():
        take(tap_far.at[pl.ds(0, TAP_TILES - 1)], sems.at[17])
        take(tap_far.at[pl.ds(0, TAP_TILES - 1)], sems.at[14])
        take(tap_far.at[pl.ds(0, place.fars - 1)], sems.at[16])

    @pl.when(jnp.logical_not(owner))
    def _():
        take(tap_far.at[pl.ds(0, TAP_TILES)], sems.at[17])
        take(tap_far.at[pl.ds(0, TAP_TILES)], sems.at[14])

    for k in range(1, place.nears):
        send(tap_all.at[place.near], tap_all.at[place.near], sems, 18, place.near_dev(k)[1])

    take(coarse_in.at[pl.ds(0, cols - 1)], sems.at[11])
    for tg in range(width // 128):
        for pg in range(lines // 8):
            parts = swap_blocks([
                coarse_in[tg * 8 + k, :, pg * 128 : (pg + 1) * 128].astype(F32) for k in range(8)
            ])
            for k in range(8):
                cot32[tg, pl.ds(pg * 8 + k, outs, stride=lines), :] = parts[k]
        coarse_ref[:, :, tg * 128 : (tg + 1) * 128] = (
            cot32[tg].reshape(outs, lines, 128).astype(BF16)
        )
    take(tap_near.at[pl.ds(0, place.nears - 1)], sems.at[19])
    for i in range(2 * radius + 1):
        for b in range(NEAR_X):
            tile = [
                tap_all[(g // TAP_TILES) * NEAR_X + b, g % TAP_TILES] for g in (2 * i, 2 * i + 1)
            ]
            line = jnp.concatenate(tile, axis=0)[: 2 * radius + 1]
            grad_tap_ref[i, :, b * 128 : (b + 1) * 128] = line
    drain_rim(place, pieces, rim_sems)
    take(near_buf.at[pl.ds(0, place.nears - 1)], sems.at[2])
    take(far_buf.at[pl.ds(0, place.fars - 1)], sems.at[4])
    take(near_sum.at[pl.ds(0, place.nears - 1)], sems.at[6])
    take(far_sum.at[pl.ds(0, place.fars - 1)], sems.at[8])
    take(coarse_in.at[pl.ds(0, cols - 1)], sems.at[10])
    take(tap_near.at[pl.ds(0, place.nears - 1)], sems.at[12])
    take(tap_near.at[pl.ds(0, place.nears - 1)], sems.at[18])


def per_device(
    features, dw_kernel, batchnorm_gain, batchnorm_offset, w_in, b_in, w_out, b_out,
    layer_scale, w_down, b_down, cotangent,
):
    rows, cols = lax.axis_size("rows"), lax.axis_size("cols")
    tile_h, tile_w, channels = features.shape
    radius = (dw_kernel.shape[0] - 1) // 2
    pixels = tile_h * tile_w
    tables = [jnp.asarray(t) for t in dft_tables(tile_h, tile_w, radius)]
    groups = tile_w // GROUP
    outs, lines, width = cotangent.shape
    hidden = w_in.shape[1]
    far = (
        features.reshape(pixels, channels),
        features.reshape(tile_h, groups, GROUP, channels),
        cotangent,
        dw_kernel,
        *tables,
        w_down.reshape(4, channels, w_down.shape[-1]),
        jnp.asarray(phase_table(tile_w)),
        w_in,
        w_out,
    )
    near = tuple(
        v.reshape(1, -1)
        for v in (batchnorm_gain, batchnorm_offset, b_in, b_out, layer_scale, b_down)
    )
    stats = (2 * channels // 128, 128)
    nears, fars = rows * NEAR_X, cols // NEAR_X
    vm = pltpu.VMEM
    scratch = [vm(a.shape, BF16) for k, a in enumerate(far) if k != 1]
    scratch += [
        vm((width // 128, outs * lines, 128), F32),
        vm((cols, outs, lines * lines), BF16),
        vm((cols, outs, lines * lines), BF16),
        vm((cols, outs, lines * lines), BF16),
        vm((CHUNK, channels), BF16),
        vm((2 * HALF, channels), F32),
        vm((2 * HALF, channels), BF16),
        vm((2 * HALF, channels), F32),
        vm((2 * HALF, channels), F32),
        vm((pixels, channels), F32),
        vm((pixels, channels), BF16),
        vm((pixels, channels), F32),
        vm((pixels, hidden), BF16),
        vm((2, radius, groups, GROUP, channels), BF16),
        vm((2, tile_h, GROUP, channels), BF16),
        vm((4, radius, GROUP, channels), BF16),
        vm((tables[1].shape[1], channels), BF16),
        vm((4, pixels // 4, channels), BF16),
        vm((tile_h, groups, GROUP, channels), BF16),
        vm((nears,) + stats, F32),
        vm((fars,) + stats, F32),
        vm((nears,) + stats, F32),
        vm((fars,) + stats, F32),
        vm(stats, F32),
        vm(stats, F32),
        vm(stats, F32),
        vm(stats, F32),
        vm((TAP_ROWS // 8, 8, channels), F32),
        vm((nears, TAP_TILES, 8, 128), F32),
        vm((TAP_TILES, 8, 128), F32),
        vm((fars, 8, 128), F32),
        vm((8, 128), F32),
        vm((nears, TAP_TILES, 8, 128), F32),
        pltpu.SemaphoreType.DMA((12,)),
        pltpu.SemaphoreType.DMA((16,)),
        pltpu.SemaphoreType.DMA((20,)),
    ]
    coarse, grad_input, grad_kernel = pl.pallas_call(
        functools.partial(step_kernel, rows, cols, radius),
        out_shape=(
            jax.ShapeDtypeStruct(cotangent.shape, BF16),
            jax.ShapeDtypeStruct((pixels, channels), BF16),
            jax.ShapeDtypeStruct(dw_kernel.shape, F32),
        ),
        in_specs=[pl.BlockSpec(memory_space=pl.ANY)] * len(far)
        + [pl.BlockSpec(memory_space=pltpu.VMEM)] * len(near),
        out_specs=[pl.BlockSpec(memory_space=pltpu.VMEM)] * 3,
        scratch_shapes=scratch,
        compiler_params=pltpu.CompilerParams(
            collective_id=1, has_side_effects=True, vmem_limit_bytes=67043328
        ),
        name="step",
    )(*far, *near)
    return coarse, grad_input.reshape(features.shape), grad_kernel


def solution(mesh):
    in_specs = (
        P("rows", "cols", None),
        P(),
        P(),
        P(),
        P(),
        P(),
        P(),
        P(),
        P(),
        P(),
        P(),
        P("cols", "rows", None),
    )
    out_specs = (P("cols", "rows", None), P("rows", "cols", None), P())
    return jax.shard_map(
        per_device, mesh=mesh, in_specs=in_specs, out_specs=out_specs, check_vma=False
    )
```

time: 244 us -> 105 us (0.43)
  the two profiles are of different devices: /device:TPU:24 before, /device:TPU:1 now
where the time goes in v1:
time: 105 us
  Pallas kernels  98.6 us (94%)
  local copies, waits for them, and re-layouts  5.96 us (6%)
    pallas_call x1, Pallas kernels, per_device(): pl.pallas_call(functools.partial(step_kernel, rows, cols, radius), out_sh...  98.6 us
    unnamed x3, local copies, waits for them, and re-layouts  5.96 us

profile of v1, /device:TPU:1, one launch (start us, length us, event | category | flops | bytes accessed | tf_op | source)
XLA Modules:
  0.0 105.2 jit_solution(974846179319767759)
XLA Ops:
  0.6 98.6 %step.1 = (bf16[32,16,512]{2,1,0:T(8,128)(2,1)}, bf16[1024,512]{1,0:T(8,128)(2,1)}, f32[13,13,512]{2,1,0:T(8,128)}) custom-call(bf16[1024,512]{1,0:T(8,128)(2,1)} %bitcast.10, bf16[32,4,8,512]{3,2,1,0:T(8,128)(2,1)} %bitcast.11, bf16[32,16,512]{2,1,0:T(8,128)(2,1)} %cot_hbm.1, bf16[13,13,512]{2,1,0:T(8,128)(2,1)} %tap_hbm.1, ...), custom_call_target="tpu_custom_call" | custom-call | tf_op jit(solution)/shard_map/step/pallas_call | solution.py:629
  99.2 1.9 %copy.24 = bf16[32,16,512]{2,1,0:T(8,128)(2,1)} copy(bf16[32,16,512]{2,1,0:T(8,128)(2,1)} %get-tuple-element.12) | data formatting | bytes 1048576
  101.1 2.3 %copy.25 = bf16[32,32,512]{2,1,0:T(8,128)(2,1)} copy(bf16[32,32,512]{2,1,0:T(8,128)(2,1)} %bitcast.13) | data formatting | bytes 2097152
  103.4 1.8 %copy.26 = f32[13,13,512]{2,1,0:T(8,128)} copy(f32[13,13,512]{2,1,0:T(8,128)} %get-tuple-element.14) | data formatting | bytes 692224

commit v2 on v1

--- a/solution.py
+++ b/solution.py
@@ -12,11 +12,11 @@
 F32 = jnp.float32
 BF16 = jnp.bfloat16
 NEAR_X = 4
-GROUP = 8
+CORNER = 48
 HALF = 1024
 TAP_LINE = 16
-TAP_TILES = 7
-TAP_ROWS = 4 * TAP_TILES * 8
+TAP_TILES = 4
+TAP_ROWS = 4 * TAP_TILES * TAP_LINE
 GELU_A, GELU_B = 0.7978845608028654, 0.044715
 CHUNK = 256
 
@@ -68,14 +68,20 @@
         return table
 
     inner = [(h, w) for h in range(tile_h) for w in range(tile_w)]
-    wests = range(-GROUP, 0)
-    easts = range(tile_w, tile_w + GROUP)
+    wests = range(-radius, 0)
+    easts = range(tile_w, tile_w + radius)
     norths = range(-radius, 0)
     souths = range(tile_h, tile_h + radius)
     rim = [(h, w) for hs in (norths, souths) for h in hs for w in range(tile_w)]
     rim += [(h, w) for ws in (wests, easts) for h in range(tile_h) for w in ws]
-    rim += [(h, w) for hs in (norths, souths) for ws in (wests, easts) for h in hs for w in ws]
-    kept = np.asarray([-radius <= w < tile_w + radius for _, w in rim])
+    kept = [True] * len(rim)
+    for hs in (norths, souths):
+        for ws in (wests, easts):
+            part = [(h, w) for h in hs for w in ws]
+            spare = CORNER - len(part)
+            rim += part + [(0, 0)] * spare
+            kept += [True] * len(part) + [False] * spare
+    kept = np.asarray(kept, np.float64)
     taps = [(i, j) for i in range(-radius, radius + 1) for j in range(-radius, radius + 1)]
     both = balanced(np.concatenate([rows(inner), rows(rim) * kept[None]], axis=1))
     count = len(inner)
@@ -98,6 +104,22 @@
         for w in range(tile_w):
             plane = (h % 2) * 2 + w % 2
             table[plane * 64 + (h // 2) * (tile_w // 2) + w // 2, h * tile_w + w] = 1.0
+    return table.astype(jnp.bfloat16)
+
+
+@functools.lru_cache(maxsize=None)
+def border_table(tile_h, tile_w, radius):
+    first, last = range(radius), range(tile_w - radius, tile_w)
+    top, bottom = range(radius), range(tile_h - radius, tile_h)
+    picks = [(h, w) for ws in (last, first) for h in range(tile_h) for w in ws]
+    for hs in (bottom, top):
+        for ws in (last, first):
+            part = [(h, w) for h in hs for w in ws]
+            picks += part + [None] * (CORNER - len(part))
+    table = np.zeros((len(picks), tile_h * tile_w), np.float32)
+    for row, pick in enumerate(picks):
+        if pick is not None:
+            table[row, pick[0] * tile_w + pick[1]] = 1.0
     return table.astype(jnp.bfloat16)
 
 
@@ -191,20 +213,17 @@
     pltpu.make_async_copy(ref, ref, sem).wait()
 
 
-def rim_pieces(block, radius, tb, lr, corner):
-    lines, groups = block.shape[0], block.shape[1]
-    south, north = pl.ds(lines - radius, radius), pl.ds(0, radius)
-    last = groups - 1
-    return (
-        (block.at[south], tb.at[0]),
-        (block.at[north], tb.at[1]),
-        (block.at[:, last], lr.at[0]),
-        (block.at[:, 0], lr.at[1]),
-        (block.at[south, last], corner.at[0]),
-        (block.at[south, 0], corner.at[1]),
-        (block.at[north, last], corner.at[2]),
-        (block.at[north, 0], corner.at[3]),
-    )
+def rim_pieces(tile, border, rim, lines, strip):
+    pixels = tile.shape[0]
+    out = [
+        (tile.at[pl.ds(pixels - lines, lines)], rim.at[pl.ds(0, lines)]),
+        (tile.at[pl.ds(0, lines)], rim.at[pl.ds(lines, lines)]),
+    ]
+    at, to = 0, 2 * lines
+    for size in (strip, strip, CORNER, CORNER, CORNER, CORNER):
+        out.append((border.at[pl.ds(at, size)], rim.at[pl.ds(to, size)]))
+        at, to = at + size, to + size
+    return tuple(out)
 
 
 def start_rim(place, pieces, sems):
@@ -214,7 +233,7 @@
             send(src, dst, sems, 2 * k, place.rim_dev(dr, dc))
 
 
-def finish_rim(place, pieces, sems, tb, lr, corner, rim):
+def finish_rim(place, pieces, sems):
     for (dr, dc), (_, dst), k in zip(STEPS, pieces, range(8)):
         @pl.when(place.inside(-dr, -dc))
         def _():
@@ -223,14 +242,6 @@
         @pl.when(jnp.logical_not(place.inside(-dr, -dc)))
         def _():
             dst[...] = jnp.zeros(dst.shape, BF16)
-
-    channels = rim.shape[1]
-    at = 0
-    for ref in (tb, lr, corner):
-        count = int(np.prod(ref.shape[:-1]))
-        flat = ref[...].astype(F32).reshape(count, channels).astype(BF16)
-        rim[at : at + count] = flat
-        at += count
 
 
 def drain_rim(place, pieces, sems):
@@ -259,27 +270,27 @@
 
 def step_kernel(
     rows, cols, radius,
-    feat_hbm, feat4_hbm, cot_hbm, tap_hbm, fin_hbm, frim_hbm, ftap_hbm, fout_hbm, gtap_hbm,
-    down_hbm, phase_hbm, win_hbm, wout_hbm, gain, offset, b_in, b_out, scale, b_down,
+    feat_hbm, cot_hbm, tap_hbm, fin_hbm, frim_hbm, ftap_hbm, fout_hbm, gtap_hbm,
+    down_hbm, phase_hbm, border_hbm, win_hbm, wout_hbm, gain, offset, b_in, b_out, scale, b_down,
     coarse_ref, grad_in_ref, grad_tap_ref,
-    feat, cot, tap_raw, fin, frim, ftap, fout, gtap, down, phase, win, wout,
+    feat, cot, tap_raw, fin, frim, ftap, fout, gtap, down, phase, choose, win, wout,
     cot32, spread, cot_in, coarse_in, taps, tap_spec, mixed, spec, own, conv, grad, xgrad, act,
-    tb, lr, corner, rim, planes, edge,
+    border, rim, planes,
     near_buf, far_buf, near_sum, far_sum, mine, mid, sums, sums_mid,
-    tap_part, tap_near, tap_share, tap_far, tap_piece, tap_all,
+    tap_part, tap_near, tap_share, tap_far, tap_all,
     in_sems, rim_sems, sems,
 ):
     place = Place(rows, cols)
     sources = (
         (cot_hbm, cot), (tap_hbm, tap_raw), (ftap_hbm, ftap), (feat_hbm, feat), (fin_hbm, fin),
         (frim_hbm, frim), (fout_hbm, fout), (down_hbm, down), (phase_hbm, phase),
-        (win_hbm, win), (wout_hbm, wout), (gtap_hbm, gtap),
+        (win_hbm, win), (wout_hbm, wout), (gtap_hbm, gtap), (border_hbm, choose),
     )
     loads = [
         pltpu.make_async_copy(src, dst, in_sems.at[k]) for k, (src, dst) in enumerate(sources)
     ]
-    for load in loads:
-        load.start()
+    for k in (3, 12, 0, 1, 2, 4, 5, 6, 7, 8, 10, 9, 11):
+        loads[k].start()
     place.greet()
 
     outs, lines, width = cot.shape
@@ -289,6 +300,17 @@
     area = (2 * lines + 2 * radius) * (side + 2 * radius)
     everything = float(pixels * rows * cols)
     zero = jnp.zeros((1, channels), F32)
+    strip = 2 * lines * radius
+    pieces = rim_pieces(feat, border, rim, radius * side, strip)
+
+    def cut_border():
+        @pl.loop(0, border.shape[0] // strip)
+        def _(m):
+            border[rows_of(m, strip)] = fdot(choose[rows_of(m, strip)], feat[...]).astype(BF16)
+
+    loads[3].wait()
+    loads[12].wait()
+    cut_border()
 
     loads[0].wait()
     for tg in range(width // 128):
@@ -300,12 +322,7 @@
             for k in range(8):
                 spread[tg * 8 + k, :, pg * 128 : (pg + 1) * 128] = parts[k].astype(BF16)
     place.met()
-    pieces = rim_pieces(feat4_hbm, radius, tb, lr, corner)
     start_rim(place, pieces, rim_sems)
-    for k in range(1, cols):
-        peer, dev = place.col_dev(k)
-        send(spread.at[peer], cot_in.at[place.c], sems, 0, dev)
-    cot_in[place.c] = spread[place.c]
 
     loads[1].wait()
     loads[2].wait()
@@ -317,14 +334,17 @@
     def _(m):
         tap_spec[rows_of(m)] = fdot(ftap[rows_of(m)], taps[...])
 
-    loads[3].wait()
     loads[4].wait()
 
     @pl.loop(0, 2 * HALF // CHUNK)
     def _(m):
         spec[rows_of(m)] = fdot(fin[rows_of(m)], feat[...])
 
-    finish_rim(place, pieces, rim_sems, tb, lr, corner, rim)
+    finish_rim(place, pieces, rim_sems)
+    for k in range(1, cols):
+        peer, dev = place.col_dev(k)
+        send(spread.at[peer], cot_in.at[place.c], sems, 0, dev)
+    cot_in[place.c] = spread[place.c]
     loads[5].wait()
 
     @pl.loop(0, HALF // CHUNK)
@@ -391,15 +411,21 @@
         normed = (xhat * gain[...] + offset[...]).astype(BF16)
         scaled = (scale[...] * grad[at].astype(F32)).astype(BF16)
         back = jnp.zeros((CHUNK, channels), F32)
-        for j in range(hidden // step):
-            cut = slice(j * step, (j + 1) * step)
-            v = fdot(normed, win[:, cut]) + b_in[:, cut]
-            act_grad = ndot(scaled, wout[cut])
+        cuts = [slice(j, j + step) for j in range(0, hidden, step)]
+
+        def enter(cut):
+            return fdot(normed, win[:, cut]) + b_in[:, cut], ndot(scaled, wout[cut])
+
+        ready = enter(cuts[0])
+        for cut, after in zip(cuts, cuts[1:] + [None]):
+            v, act_grad = ready
+            if after is not None:
+                ready = enter(after)
             square = v * v
-            t = jnp.tanh(GELU_A * v * (1.0 + GELU_B * square))
-            gate = 0.5 * (1.0 + t)
+            gate = 0.5 * jnp.tanh(v * (GELU_A + (GELU_A * GELU_B) * square)) + 0.5
             act[at, cut] = (v * gate).astype(BF16)
-            slope = gate + (0.5 * GELU_A) * v * (1.0 - t * t) * (1.0 + (3.0 * GELU_B) * square)
+            bend = v * (2.0 * GELU_A + (6.0 * GELU_A * GELU_B) * square)
+            slope = gate * ((1.0 - gate) * bend + 1.0)
             back = back + ndot((act_grad * slope).astype(BF16), win[:, cut])
         back = back * gain[...]
         xgrad[at] = back
@@ -430,25 +456,15 @@
     for ab in range(4):
         flat = flat + fdot(planes[ab], down[ab])
     spread[...] = flat.T.astype(BF16).reshape(cols, outs, lines * lines)
-    for k in range(1, cols):
-        peer, dev = place.col_dev(k)
-        send(spread.at[peer], coarse_in.at[place.c], sems, 10, dev)
-    coarse_in[place.c] = spread[place.c]
     take(far_sum.at[pl.ds(0, place.fars - 1)], sems.at[9])
     both = jnp.sum(far_sum[...], axis=0) * (1.0 / everything)
     level, slant = row_of(both[:half]), row_of(both[half:])
 
-    groups = edge.shape[1]
     for k in range(parts_n):
         at = slice(k * CHUNK, (k + 1) * CHUNK)
         xhat = (conv[at] - mean) * inverse
-        block = inverse * (xgrad[at] - level - xhat * slant)
-        feat[at] = block.astype(BF16)
-        tall_lines = CHUNK // side
-        edge[k * tall_lines : (k + 1) * tall_lines] = block.reshape(
-            tall_lines, groups, GROUP, channels
-        ).astype(BF16)
-    pieces = rim_pieces(edge, radius, tb, lr, corner)
+        feat[at] = (inverse * (xgrad[at] - level - xhat * slant)).astype(BF16)
+    cut_border()
     start_rim(place, pieces, rim_sems)
 
     @pl.loop(0, HALF // CHUNK)
@@ -462,7 +478,7 @@
 
     loads[11].wait()
     norm = 1.0 / (area * float(np.sqrt(everything)))
-    tap_part[...] = (fdot(gtap[...], mixed[...]) * norm).reshape(tap_part.shape)
+    tap_part[...] = (fdot(gtap[...], mixed[...]) * norm).reshape(tap_part.shape).astype(BF16)
 
     def tap_block(index):
         start = pl.multiple_of((index % NEAR_X) * 128, 128)
@@ -473,7 +489,11 @@
         send(tap_block(peer), tap_near.at[place.near], sems, 12, dev)
     tap_near[place.near] = tap_block(place.near)[...]
 
-    finish_rim(place, pieces, rim_sems, tb, lr, corner, rim)
+    finish_rim(place, pieces, rim_sems)
+    for k in range(1, cols):
+        peer, dev = place.col_dev(k)
+        send(spread.at[peer], coarse_in.at[place.c], sems, 10, dev)
+    coarse_in[place.c] = spread[place.c]
 
     @pl.loop(0, HALF // CHUNK)
     def _(m):
@@ -485,48 +505,21 @@
         mixed[im] = (gr * ki + gi * kr).astype(BF16)
 
     take(tap_near.at[pl.ds(0, place.nears - 1)], sems.at[13])
-    tap_share[...] = jnp.sum(tap_near[...], axis=0)
-    owner = place.far < TAP_TILES
+    tap_share[...] = jnp.sum(tap_near[...].astype(F32), axis=0).astype(BF16)
     for k in range(1, place.fars):
-        peer, dev = place.far_dev(k)
-
-        @pl.when(peer < TAP_TILES)
-        def _():
-            send(tap_share.at[peer], tap_far.at[place.far], sems, 14, dev)
-
-    def spread_out(m):
-        at = slice(m * CHUNK, (m + 1) * CHUNK)
+        send(tap_share, tap_far.at[place.far], sems, 14, place.far_dev(k)[1])
+    tap_far[place.far] = tap_share[...]
+
+    @pl.loop(0, parts_n)
+    def _(m):
+        at = rows_of(m)
         block = fdot(fout[at], mixed[...]) * (1.0 / area)
         grad_in_ref[at] = (grad[at].astype(F32) + block).astype(BF16)
 
-    for m in range(parts_n // 2):
-        spread_out(m)
-
-    @pl.when(owner)
-    def _():
-        tap_far[place.far] = tap_share[place.far]
-        take(tap_far.at[pl.ds(0, place.fars - 1)], sems.at[15])
-        tap_piece[...] = jnp.sum(tap_far[...], axis=0)
-        for k in range(1, place.fars):
-            send(tap_piece, tap_all.at[place.near, place.far], sems, 16, place.far_dev(k)[1])
-        tap_all[place.near, place.far] = tap_piece[...]
-
-    for m in range(parts_n // 2, parts_n):
-        spread_out(m)
-
-    @pl.when(owner)
-    def _():
-        take(tap_far.at[pl.ds(0, TAP_TILES - 1)], sems.at[17])
-        take(tap_far.at[pl.ds(0, TAP_TILES - 1)], sems.at[14])
-        take(tap_far.at[pl.ds(0, place.fars - 1)], sems.at[16])
-
-    @pl.when(jnp.logical_not(owner))
-    def _():
-        take(tap_far.at[pl.ds(0, TAP_TILES)], sems.at[17])
-        take(tap_far.at[pl.ds(0, TAP_TILES)], sems.at[14])
-
+    take(tap_far.at[pl.ds(0, place.fars - 1)], sems.at[15])
+    tap_all[place.near] = jnp.sum(tap_far[...].astype(F32), axis=0).astype(BF16)
     for k in range(1, place.nears):
-        send(tap_all.at[place.near], tap_all.at[place.near], sems, 18, place.near_dev(k)[1])
+        send(tap_all.at[place.near], tap_all.at[place.near], sems, 16, place.near_dev(k)[1])
 
     take(coarse_in.at[pl.ds(0, cols - 1)], sems.at[11])
     for tg in range(width // 128):
@@ -539,14 +532,11 @@
         coarse_ref[:, :, tg * 128 : (tg + 1) * 128] = (
             cot32[tg].reshape(outs, lines, 128).astype(BF16)
         )
-    take(tap_near.at[pl.ds(0, place.nears - 1)], sems.at[19])
+    take(tap_near.at[pl.ds(0, place.nears - 1)], sems.at[17])
     for i in range(2 * radius + 1):
         for b in range(NEAR_X):
-            tile = [
-                tap_all[(g // TAP_TILES) * NEAR_X + b, g % TAP_TILES] for g in (2 * i, 2 * i + 1)
-            ]
-            line = jnp.concatenate(tile, axis=0)[: 2 * radius + 1]
-            grad_tap_ref[i, :, b * 128 : (b + 1) * 128] = line
+            line = tap_all[(i // TAP_TILES) * NEAR_X + b, i % TAP_TILES].astype(F32)
+            grad_tap_ref[i, :, b * 128 : (b + 1) * 128] = line[: 2 * radius + 1]
     drain_rim(place, pieces, rim_sems)
     take(near_buf.at[pl.ds(0, place.nears - 1)], sems.at[2])
     take(far_buf.at[pl.ds(0, place.fars - 1)], sems.at[4])
@@ -554,7 +544,26 @@
     take(far_sum.at[pl.ds(0, place.fars - 1)], sems.at[8])
     take(coarse_in.at[pl.ds(0, cols - 1)], sems.at[10])
     take(tap_near.at[pl.ds(0, place.nears - 1)], sems.at[12])
-    take(tap_near.at[pl.ds(0, place.nears - 1)], sems.at[18])
+    take(tap_far.at[pl.ds(0, place.fars - 1)], sems.at[14])
+    take(tap_near.at[pl.ds(0, place.nears - 1)], sems.at[16])
+
+
+def hand_over(a_in, b_in, c_in, a_out, b_out, c_out, a, b, c, sems):
+    enter = [
+        pltpu.make_async_copy(src, dst, sems.at[k])
+        for k, (src, dst) in enumerate(((a_in, a), (b_in, b), (c_in, c)))
+    ]
+    leave = [
+        pltpu.make_async_copy(src, dst, sems.at[3 + k])
+        for k, (src, dst) in enumerate(((a, a_out), (b, b_out), (c, c_out)))
+    ]
+    for copy in enter:
+        copy.start()
+    for arrive, go in zip(enter, leave):
+        arrive.wait()
+        go.start()
+    for copy in leave:
+        copy.wait()
 
 
 def per_device(
@@ -566,17 +575,16 @@
     radius = (dw_kernel.shape[0] - 1) // 2
     pixels = tile_h * tile_w
     tables = [jnp.asarray(t) for t in dft_tables(tile_h, tile_w, radius)]
-    groups = tile_w // GROUP
     outs, lines, width = cotangent.shape
     hidden = w_in.shape[1]
     far = (
         features.reshape(pixels, channels),
-        features.reshape(tile_h, groups, GROUP, channels),
         cotangent,
         dw_kernel,
         *tables,
         w_down.reshape(4, channels, w_down.shape[-1]),
         jnp.asarray(phase_table(tile_w)),
+        jnp.asarray(border_table(tile_h, tile_w, radius)),
         w_in,
         w_out,
     )
@@ -587,7 +595,7 @@
     stats = (2 * channels // 128, 128)
     nears, fars = rows * NEAR_X, cols // NEAR_X
     vm = pltpu.VMEM
-    scratch = [vm(a.shape, BF16) for k, a in enumerate(far) if k != 1]
+    scratch = [vm(a.shape, BF16) for a in far]
     scratch += [
         vm((width // 128, outs * lines, 128), F32),
         vm((cols, outs, lines * lines), BF16),
@@ -602,12 +610,9 @@
         vm((pixels, channels), BF16),
         vm((pixels, channels), F32),
         vm((pixels, hidden), BF16),
-        vm((2, radius, groups, GROUP, channels), BF16),
-        vm((2, tile_h, GROUP, channels), BF16),
-        vm((4, radius, GROUP, channels), BF16),
+        vm((far[-3].shape[0], channels), BF16),
         vm((tables[1].shape[1], channels), BF16),
         vm((4, pixels // 4, channels), BF16),
-        vm((tile_h, groups, GROUP, channels), BF16),
         vm((nears,) + stats, F32),
         vm((fars,) + stats, F32),
         vm((nears,) + stats, F32),
@@ -616,17 +621,16 @@
         vm(stats, F32),
         vm(stats, F32),
         vm(stats, F32),
-        vm((TAP_ROWS // 8, 8, channels), F32),
-        vm((nears, TAP_TILES, 8, 128), F32),
-        vm((TAP_TILES, 8, 128), F32),
-        vm((fars, 8, 128), F32),
-        vm((8, 128), F32),
-        vm((nears, TAP_TILES, 8, 128), F32),
-        pltpu.SemaphoreType.DMA((12,)),
+        vm((TAP_ROWS // TAP_LINE, TAP_LINE, channels), BF16),
+        vm((nears, TAP_TILES, TAP_LINE, 128), BF16),
+        vm((TAP_TILES, TAP_LINE, 128), BF16),
+        vm((fars, TAP_TILES, TAP_LINE, 128), BF16),
+        vm((nears, TAP_TILES, TAP_LINE, 128), BF16),
+        pltpu.SemaphoreType.DMA((13,)),
         pltpu.SemaphoreType.DMA((16,)),
-        pltpu.SemaphoreType.DMA((20,)),
+        pltpu.SemaphoreType.DMA((18,)),
     ]
-    coarse, grad_input, grad_kernel = pl.pallas_call(
+    results = pl.pallas_call(
         functools.partial(step_kernel, rows, cols, radius),
         out_shape=(
             jax.ShapeDtypeStruct(cotangent.shape, BF16),
@@ -642,6 +646,14 @@
         ),
         name="step",
     )(*far, *near)
+    coarse, grad_input, grad_kernel = pl.pallas_call(
+        hand_over,
+        out_shape=tuple(jax.ShapeDtypeStruct(a.shape, a.dtype) for a in results),
+        in_specs=[pl.BlockSpec(memory_space=pl.ANY)] * 3,
+        out_specs=[pl.BlockSpec(memory_space=pl.ANY)] * 3,
+        scratch_shapes=[vm(a.shape, a.dtype) for a in results] + [pltpu.SemaphoreType.DMA((6,))],
+        name="hand_over",
+    )(*results)
     return coarse, grad_input.reshape(features.shape), grad_kernel
 
 

time: 105 us -> 92.2 us (0.88)
  Pallas kernels: 98.6 us -> 90.7 us
  local copies, waits for them, and re-layouts: 5.96 us -> 0 us
    pallas_call x1, Pallas kernels: 98.6 us -> 88.1 us  [per_device(): pl.pallas_call(functools.partial(step_kernel, rows, cols, radius), out_sh...]
    unnamed x3 -> x0, local copies, waits for them, and re-layouts: 5.96 us -> none
    pallas_call x0 -> x1, Pallas kernels: none -> 2.54 us  [per_device(): pl.pallas_call(hand_over, out_shape=tuple((jax.ShapeDtypeStruct(a.shape,...]
where the time goes in v2:
time: 92.2 us; the launch traced here: 91.5 us
  Pallas kernels  90.7 us (98%)
    pallas_call x1, Pallas kernels, per_device(): pl.pallas_call(functools.partial(step_kernel, rows, cols, radius), out_sh...  88.1 us
    pallas_call x1, Pallas kernels, per_device(): pl.pallas_call(hand_over, out_shape=tuple((jax.ShapeDtypeStruct(a.shape,...  2.54 us

profile of v2, /device:TPU:1, one launch (start us, length us, event | category | flops | bytes accessed | tf_op | source)
XLA Modules:
  0.0 91.5 jit_solution(18218947655421961955)
XLA Ops:
  0.6 88.1 %step.1 = (bf16[32,16,512]{2,1,0:T(8,128)(2,1)}, bf16[1024,512]{1,0:T(8,128)(2,1)}, f32[13,13,512]{2,1,0:T(8,128)}) custom-call(bf16[1024,512]{1,0:T(8,128)(2,1)} %bitcast.10, bf16[32,16,512]{2,1,0:T(8,128)(2,1)} %cot_hbm.1, bf16[13,13,512]{2,1,0:T(8,128)(2,1)} %tap_hbm.1, bf16[2048,1024]{1,0:T(8,128)(2,1)} %constant.14.clone.fin_hbm, ...), custom_call_target="tpu_custom_call" | custom-call | tf_op jit(solution)/shard_map/step/pallas_call | solution.py:633
  88.8 2.5 %hand_over.1 = (bf16[32,16,512]{2,1,0:T(8,128)(2,1)}, bf16[1024,512]{1,0:T(8,128)(2,1)}, f32[13,13,512]{2,1,0:T(8,128)}) custom-call(bf16[32,16,512]{2,1,0:T(8,128)(2,1)} %get-tuple-element.9.a_in, bf16[1024,512]{1,0:T(8,128)(2,1)} %get-tuple-element.10.b_in, f32[13,13,512]{2,1,0:T(8,128)} %get-tuple-element.11.c_in), custom_call_target="tpu_custom_call" | custom-call | tf_op jit(solution)/shard_map/hand_over/pallas_call | solution.py:649
